TPU v7x, 256 devices: a whole 4x4x8 slice. The times are simulated.
256 devices in a mesh: depth: 2 (over core), pos: 128 (over x, z, y).
Axes of the slice: x: 4, y: 4, z: 8, core: 2. Of those that a mesh axis runs over, the one named last changes fastest.
Arguments:
- object_field: bfloat16 [2, 2, 2048, 32768], P('depth', None, None, 'pos'), may hold values from -4.1875 to 4.1875
- probe: bfloat16 [4, 2, 256, 256], replicated, may hold values from -4.1875 to 4.1875
- prop_phase: float32 [256, 256], replicated, may hold values from -3.140625 to 3.140625
- measured: float32 [256, 256, 256], P('pos'), may hold values from 0 to 8
- positions: int32 [256, 2], replicated, may hold values from 0 to 32512, as said below
Outputs:
- object_grad: bfloat16 [2, 2, 2048, 32768], P('depth', None, None, 'pos')
Inputs may be any that keep to these rules, and one draw needn't show every extreme that they name: `positions`: row r holds (row offset, column offset). For the block b = r // 2, column offsets lie from b * 256 to b * 256 + 255; in the last block they equal b * 256. Row offsets lie from 0 to 1792. Row 0 is (0, 0).
All inputs are finite; a program needn't handle non-finite values.
Results may differ from a plain program's by a relative error of at most 0.019.
Values may be sent and summed in bfloat16 or wider, within the bound.
A program may use at most 64 MiB of HBM per device.

v0:
```python
import math

import jax
import jax.numpy as jnp
from jax import lax
from jax.sharding import PartitionSpec as P


def shifted(shard, axis, by):
    devices = lax.axis_size(axis)
    pairs = [(i, i + by) for i in range(devices) if 0 <= i + by < devices]
    return lax.ppermute(shard, axis, pairs)


def dft_tables(frame):
    ramp = jnp.arange(frame, dtype=jnp.int32)
    phases = ramp[:, None] * ramp[None, :] % frame
    angles = phases.astype(jnp.float32) * (2.0 * math.pi / frame)
    factor = 1.0 / math.sqrt(frame)
    return (
        (jnp.cos(angles) * factor).astype(jnp.bfloat16),
        (-jnp.sin(angles) * factor).astype(jnp.bfloat16),
    )


def left_mult(table, values):
    return jnp.einsum("ab,nmbc->nmac", table, values, preferred_element_type=jnp.float32)


def right_mult(values, table):
    return jnp.einsum("nmab,bc->nmac", values, table, preferred_element_type=jnp.float32)


def transform(real_in, imag_in, fourier_table_real, fourier_table_imaginary):
    in_r = real_in.astype(jnp.bfloat16)
    in_i = imag_in.astype(jnp.bfloat16)
    mid_r = (left_mult(fourier_table_real, in_r) - left_mult(fourier_table_imaginary, in_i)).astype(
        jnp.bfloat16
    )
    mid_i = (left_mult(fourier_table_real, in_i) + left_mult(fourier_table_imaginary, in_r)).astype(
        jnp.bfloat16
    )
    out_r = right_mult(mid_r, fourier_table_real) - right_mult(mid_i, fourier_table_imaginary)
    out_i = right_mult(mid_r, fourier_table_imaginary) + right_mult(mid_i, fourier_table_real)
    return (out_r, out_i)


def forward_front(
    patch_r, patch_i, probe, kern_r, kern_i, fourier_table_real, fourier_table_imaginary
):
    obj_r = patch_r.astype(jnp.float32)[:, None]
    obj_i = patch_i.astype(jnp.float32)[:, None]
    probe_r = probe[:, 0].astype(jnp.float32)[None]
    probe_i = probe[:, 1].astype(jnp.float32)[None]
    wave_r = probe_r * obj_r - probe_i * obj_i
    wave_i = probe_r * obj_i + probe_i * obj_r
    spectrum_real, spectrum_imaginary = transform(
        wave_r, wave_i, fourier_table_real, fourier_table_imaginary
    )
    return jnp.stack(
        [
            (spectrum_real * kern_r - spectrum_imaginary * kern_i).astype(jnp.bfloat16),
            (spectrum_real * kern_i + spectrum_imaginary * kern_r).astype(jnp.bfloat16),
        ]
    )


def backward_tail(spectra, patch_r, patch_i, measured, fourier_table_real, fourier_table_imaginary):
    conj_i = -fourier_table_imaginary
    wave_r, wave_i = transform(spectra[0], spectra[1], fourier_table_real, conj_i)
    obj_r = patch_r.astype(jnp.float32)[:, None]
    obj_i = patch_i.astype(jnp.float32)[:, None]
    exit_r = wave_r * obj_r - wave_i * obj_i
    exit_i = wave_r * obj_i + wave_i * obj_r
    far_r, far_i = transform(exit_r, exit_i, fourier_table_real, fourier_table_imaginary)
    intensity = jnp.sum(far_r * far_r + far_i * far_i, axis=1)
    weight = ((intensity - measured) * 0.125)[:, None]
    back_r, back_i = transform(weight * far_r, weight * far_i, fourier_table_real, conj_i)
    grad_r = jnp.sum(wave_r * back_r + wave_i * back_i, axis=1)
    grad_i = jnp.sum(wave_r * back_i - wave_i * back_r, axis=1)
    adj_r = obj_r * back_r + obj_i * back_i
    adj_i = obj_r * back_i - obj_i * back_r
    out_r, out_i = transform(adj_r, adj_i, fourier_table_real, fourier_table_imaginary)
    return (
        jnp.stack([out_r.astype(jnp.bfloat16), out_i.astype(jnp.bfloat16)]),
        jnp.stack([grad_r, grad_i]),
    )


def back_front(adjoint, probe, kern_r, kern_i, fourier_table_real, fourier_table_imaginary):
    cot_r = adjoint[0].astype(jnp.float32)
    cot_i = adjoint[1].astype(jnp.float32)
    turn_r = kern_r * cot_r + kern_i * cot_i
    turn_i = kern_r * cot_i - kern_i * cot_r
    wave_r, wave_i = transform(turn_r, turn_i, fourier_table_real, -fourier_table_imaginary)
    probe_r = probe[:, 0].astype(jnp.float32)[None]
    probe_i = probe[:, 1].astype(jnp.float32)[None]
    grad_r = jnp.sum(probe_r * wave_r + probe_i * wave_i, axis=1)
    grad_i = jnp.sum(probe_r * wave_i - probe_i * wave_r, axis=1)
    return jnp.stack([grad_r, grad_i])


def local(object_field, probe, prop_phase, measured, positions):
    frame = probe.shape[-1]
    n_modes = probe.shape[0]
    count = measured.shape[0]
    fourier_table_real, fourier_table_imaginary = dft_tables(frame)
    kern_r = jnp.cos(prop_phase)
    kern_i = jnp.sin(prop_phase)
    section_idx = lax.axis_index("depth")
    pos_index = lax.axis_index("pos")
    my_positions = lax.dynamic_slice_in_dim(positions, pos_index * count, count, 0)
    rows_mine = my_positions[:, 0]
    cols_mine = my_positions[:, 1] - pos_index * frame
    my_band = object_field[0]
    height = my_band.shape[1]
    right_band = shifted(my_band, "pos", -1)
    wide_band = jnp.concatenate([my_band, right_band], axis=2)
    patches = jnp.stack(
        [
            lax.dynamic_slice(
                wide_band, (0, rows_mine[which_pos], cols_mine[which_pos]), (2, frame, frame)
            )
            for which_pos in range(count)
        ]
    )
    patch_r = patches[:, 0]
    patch_i = patches[:, 1]

    def spec_zeros(rows_n):
        return jnp.zeros((2, rows_n, n_modes, frame, frame), jnp.bfloat16)

    def grad_zeros(rows_n):
        return jnp.zeros((2, rows_n, frame, frame), jnp.float32)

    def front_pass():
        return forward_front(
            patch_r, patch_i, probe, kern_r, kern_i, fourier_table_real, fourier_table_imaginary
        )

    spectra = lax.cond(section_idx == 0, front_pass, lambda: spec_zeros(count))
    arrived = shifted(spectra, "depth", 1)

    def end_pass():
        return backward_tail(
            arrived, patch_r, patch_i, measured, fourier_table_real, fourier_table_imaginary
        )

    adjoint, grad_end = lax.cond(
        section_idx == 1, end_pass, lambda: (spec_zeros(count), grad_zeros(count))
    )
    returned = shifted(adjoint, "depth", -1)

    def front_back():
        return back_front(
            returned, probe, kern_r, kern_i, fourier_table_real, fourier_table_imaginary
        )

    grads = lax.cond(section_idx == 0, front_back, lambda: grad_end)
    buffer = jnp.zeros((2, height, 2 * frame), jnp.float32)
    for which_pos in range(count):
        corner = (0, rows_mine[which_pos], cols_mine[which_pos])
        current = lax.dynamic_slice(buffer, corner, (2, frame, frame))
        buffer = lax.dynamic_update_slice(buffer, current + grads[:, which_pos], corner)
    from_left = shifted(buffer[:, :, frame:], "pos", 1)
    total = buffer[:, :, :frame] + from_left
    return total.astype(jnp.bfloat16)[None]


def solution(mesh):
    placed = (P("depth", None, None, "pos"), P(), P(), P("pos", None, None), P())
    return jax.shard_map(
        local, mesh=mesh, in_specs=placed, out_specs=P("depth", None, None, "pos"), check_vma=False
    )
```

profile of v0, /device:TPU:6, one launch (start us, length us, event | category | flops | bytes accessed | tf_op | source)
XLA Modules:
  0.0 233.8 jit_solution(5803860364663866758)
XLA Ops:
  0.0 10.6 %collective-permute-start = (bf16[2,2048,256]{2,1,0:T(8,128)(2,1)}, bf16[2,2048,256]{2,1,0:T(8,128)(2,1)S(1)}, u32[]{:S(2)}, u32[]{:S(2)}) collective-permute-start(bf16[2,2048,256]{2,1,0:T(8,128)(2,1)} %bitcast.389), channel_id=1, source_target_pairs={{1,0},{2,1},{3,2},{4,3},{5,4},{6,5},{7,6},{8,7},{9,8},{10,9},{11,1... | collective-permute-start | bytes 6291464 | tf_op jit(solution)/shard_map/ppermute | solution.py:12
  16.9 1.1 copy.43
  20.6 1.1 multiply_convert_fusion.6
  21.7 1.0 fusion.152
  22.6 33.1 %collective-permute-done = bf16[2,2048,256]{2,1,0:T(8,128)(2,1)S(1)} collective-permute-done((bf16[2,2048,256]{2,1,0:T(8,128)(2,1)}, bf16[2,2048,256]{2,1,0:T(8,128)(2,1)S(1)}, u32[]{:S(2)}, u32[]{:S(2)}) %collective-permute-start) | collective-permute-done | bytes 2097184 | tf_op jit(solution)/shard_map/ppermute | solution.py:12
  55.8 1.6 fusion.151
  58.3 12.3 %conditional.3 = (bf16[2,2,4,256,256]{4,3,2,1,0:T(8,128)(2,1)S(1)}) conditional(s32[]{:T(128)} %convert_element_type.399, () %tuple.48, (bf16[4,2,256,256]{3,2,1,0:T(8,128)(2,1)}, bf16[2,256,256]{2,1,0:T(8,128)(2,1)}, bf16[2,256,256]{2,1,0:T(8,128)(2,1)}, bf16[256,256]{1,0:T(8,128)(2,1)S(1)}, bf16[256,256]{1,0:T(8,128)(2,1)S(1)}, ...), branch_computations={%region_0.1_spmd, %region_1.2_spmd} | conditional | flops 2165047296 | bytes 60817444 | solution.py:141
  58.5 1.1 copy.47
  59.7 1.8 copy.46
  61.5 1.0 convert_element_type.95
  62.5 1.3 copy.45
  63.8 1.4 fusion.23
  69.3 1.0 fusion.4
  70.5 2.3 %copy.50 = bf16[2,2,4,256,256]{3,4,2,1,0:T(8,128)(2,1)} copy(bf16[2,2,4,256,256]{4,3,2,1,0:T(8,128)(2,1)S(1)} %get-tuple-element.254) | data formatting | bytes 4194304 | tf_op jit(solution)/shard_map/cond | solution.py:141
  72.9 1.4 collective-permute-start.1
  74.3 3.8 %collective-permute-done.1 = bf16[2,2,4,256,256]{3,4,2,1,0:T(8,128)(2,1)S(1)} collective-permute-done((bf16[2,2,4,256,256]{3,4,2,1,0:T(8,128)(2,1)}, bf16[2,2,4,256,256]{3,4,2,1,0:T(8,128)(2,1)S(1)}, u32[]{:S(2)}, u32[]{:S(2)}) %collective-permute-start.1) | collective-permute-done | bytes 2097184 | tf_op jit(solution)/shard_map/ppermute | solution.py:12
  78.2 1.6 conditional.4
  78.2 1.5 broadcast.27
  79.8 1.0 copy-done.5
  80.7 4.3 %copy.51 = bf16[2,2,4,256,256]{3,4,2,1,0:T(8,128)(2,1)} copy(bf16[2,2,4,256,256]{4,3,2,1,0:T(8,128)(2,1)} %get-tuple-element.191) | data formatting | bytes 4194304 | tf_op jit(solution)/shard_map/cond | solution.py:149
  85.0 1.3 collective-permute-start.2
  86.3 24.2 %collective-permute-done.2 = bf16[2,2,4,256,256]{3,4,2,1,0:T(8,128)(2,1)S(1)} collective-permute-done((bf16[2,2,4,256,256]{3,4,2,1,0:T(8,128)(2,1)}, bf16[2,2,4,256,256]{3,4,2,1,0:T(8,128)(2,1)S(1)}, u32[]{:S(2)}, u32[]{:S(2)}) %collective-permute-start.2) | collective-permute-done | bytes 2097184 | tf_op jit(solution)/shard_map/ppermute | solution.py:12
  110.6 5.6 %conditional.5 = (f32[2,2,256,256]{3,2,1,0:T(8,128)S(1)}) conditional(s32[]{:T(128)} %convert_element_type.399, f32[2,2,256,256]{3,2,1,0:T(8,128)S(1)} %copy-done.6, (bf16[4,2,256,256]{3,2,1,0:T(8,128)(2,1)S(1)}, f32[256,256]{0,1:T(8,128)S(1)}, bf16[2,2,4,256,256]{3,4,2,1,0:T(8,128)(2,1)S(1)}, f32[256,256]{0,1:T(8,128)S(1)}, ...), branch_computations={%region_7.8_spmd, %region_8.11_spmd} | conditional | flops 2168193024 | bytes 47185928 | solution.py:159
  114.9 1.2 add_reduce_fusion.2
  116.2 4.3 %broadcast_in_dim.4 = f32[2,2048,512]{2,1,0:T(8,128)} broadcast(f32[]{:T(128)} %constant.25.clone.1), dimensions={} | broadcast | bytes 8388612 | tf_op jit(solution)/shard_map/broadcast_in_dim | solution.py:160
  120.5 6.5 %dynamic_update_slice.6 = f32[2,2048,512]{2,1,0:T(8,128)} dynamic-update-slice(f32[2,2048,512]{2,1,0:T(8,128)} %broadcast_in_dim.4, f32[2,256,256]{2,1,0:T(8,128)S(1)} %slice_bitcast_fusion.5, s32[]{:T(128)} %constant.43.clone.1, s32[]{:T(128)S(6)} %select_n.123, s32[]{:T(128)S(6)} %select_n.124) | dynamic-update-slice | bytes 1048580 | tf_op jit(solution)/shard_map/dynamic_update_slice | solution.py:164
  127.0 1.4 fusion.138
  128.4 6.8 %dynamic_update_slice.7 = f32[2,2048,512]{2,1,0:T(8,128)} dynamic-update-slice(f32[2,2048,512]{2,1,0:T(8,128)} %dynamic_update_slice.6, f32[2,256,256]{2,1,0:T(8,128)S(1)} %fusion.138, s32[]{:T(128)} %constant.43.clone.1, s32[]{:T(128)S(6)} %select_n.125, s32[]{:T(128)S(6)} %select_n.126) | dynamic-update-slice | bytes 1048580 | tf_op jit(solution)/shard_map/dynamic_update_slice | solution.py:164
  135.2 2.6 %slice.116 = f32[2,2048,256]{2,1,0:T(8,128)S(1)} slice(f32[2,2048,512]{2,1,0:T(8,128)} %dynamic_update_slice.7), slice={[0:2], [0:2048], [256:512]} | slice | bytes 8388608 | tf_op jit(solution)/shard_map/slice | solution.py:165
  137.8 2.2 collective-permute-start.3
  140.0 91.8 %collective-permute-done.3 = f32[2,2048,256]{2,1,0:T(8,128)S(1)} collective-permute-done((f32[2,2048,256]{2,1,0:T(8,128)S(1)}, f32[2,2048,256]{2,1,0:T(8,128)S(1)}, u32[]{:S(2)}, u32[]{:S(2)}) %collective-permute-start.3) | collective-permute-done | bytes 4194336 | tf_op jit(solution)/shard_map/ppermute | solution.py:12
  231.8 2.0 fusion.137
  (42 shorter events, 11.2 us)
Async XLA Ops:
  0.0 10.6 %copy-start = (s32[256,2]{0,1:T(2,128)S(1)}, s32[256,2]{0,1:T(2,128)}, u32[]{:S(2)}) copy-start(s32[256,2]{0,1:T(2,128)} %param.15) | copy-start | bytes 6148
  0.0 55.8 %collective-permute-start = (bf16[2,2048,256]{2,1,0:T(8,128)(2,1)}, bf16[2,2048,256]{2,1,0:T(8,128)(2,1)S(1)}, u32[]{:S(2)}, u32[]{:S(2)}) collective-permute-start(bf16[2,2048,256]{2,1,0:T(8,128)(2,1)} %bitcast.389), channel_id=1, source_target_pairs={{1,0},{2,1},{3,2},{4,3},{5,4},{6,5},{7,6},{8,7},{9,8},{10,9},{11,1... | collective-permute-start | bytes 6291464 | tf_op jit(solution)/shard_map/ppermute | solution.py:12
  58.3 4.2 %copy-start.4 = (bf16[4,2,256,256]{3,2,1,0:T(8,128)(2,1)S(1)}, bf16[4,2,256,256]{3,2,1,0:T(8,128)(2,1)}, u32[]{:S(2)}) copy-start(bf16[4,2,256,256]{3,2,1,0:T(8,128)(2,1)} %get-tuple-element.194) | copy-start | bytes 3145732 | tf_op jit(solution)/shard_map/cond
  70.5 7.6 %copy-start.7 = (f32[2,256,256]{2,1,0:T(8,128)S(1)}, f32[2,256,256]{2,1,0:T(8,128)}, u32[]{:S(2)}) copy-start(f32[2,256,256]{2,1,0:T(8,128)} %param.14) | copy-start | bytes 1572868
  72.9 5.3 %collective-permute-start.1 = (bf16[2,2,4,256,256]{3,4,2,1,0:T(8,128)(2,1)}, bf16[2,2,4,256,256]{3,4,2,1,0:T(8,128)(2,1)S(1)}, u32[]{:S(2)}, u32[]{:S(2)}) collective-permute-start(bf16[2,2,4,256,256]{3,4,2,1,0:T(8,128)(2,1)} %copy.50), channel_id=1, source_target_pairs={{0,128},{1,129},{2,130},{3,131},{4,132},{5,133},{6,134},{7,135},{8... | collective-permute-start | bytes 6291464 | tf_op jit(solution)/shard_map/ppermute | solution.py:12
  79.8 1.0 copy-start.5
  80.7 29.8 %copy-start.3 = (bf16[4,2,256,256]{3,2,1,0:T(8,128)(2,1)S(1)}, bf16[4,2,256,256]{3,2,1,0:T(8,128)(2,1)}, u32[]{:S(2)}) copy-start(bf16[4,2,256,256]{3,2,1,0:T(8,128)(2,1)} %param.12) | copy-start | bytes 3145732
  80.7 29.8 %copy-start.6 = (f32[2,2,256,256]{3,2,1,0:T(8,128)S(1)}, f32[2,2,256,256]{3,2,1,0:T(8,128)}, u32[]{:S(2)}) copy-start(f32[2,2,256,256]{3,2,1,0:T(8,128)} %copy-done.5) | copy-start | bytes 3145732
  85.0 25.5 %collective-permute-start.2 = (bf16[2,2,4,256,256]{3,4,2,1,0:T(8,128)(2,1)}, bf16[2,2,4,256,256]{3,4,2,1,0:T(8,128)(2,1)S(1)}, u32[]{:S(2)}, u32[]{:S(2)}) collective-permute-start(bf16[2,2,4,256,256]{3,4,2,1,0:T(8,128)(2,1)} %copy.51), channel_id=1, source_target_pairs={{128,0},{129,1},{130,2},{131,3},{132,4},{133,5},{134,6},{135,7},{1... | collective-permute-start | bytes 6291464 | tf_op jit(solution)/shard_map/ppermute | solution.py:12
  135.2 96.7 %copy-start.2 = (f32[2,2048,512]{2,1,0:T(8,128)S(1)}, f32[2,2048,512]{2,1,0:T(8,128)}, u32[]{:S(2)}) copy-start(f32[2,2048,512]{2,1,0:T(8,128)} %dynamic_update_slice.7) | copy-start | bytes 25165828
  137.8 94.0 %collective-permute-start.3 = (f32[2,2048,256]{2,1,0:T(8,128)S(1)}, f32[2,2048,256]{2,1,0:T(8,128)S(1)}, u32[]{:S(2)}, u32[]{:S(2)}) collective-permute-start(f32[2,2048,256]{2,1,0:T(8,128)S(1)} %slice.116), channel_id=1, source_target_pairs={{0,1},{1,2},{2,3},{3,4},{4,5},{5,6},{6,7},{7,8},{8,9},{9,10},{10,1... | collective-permute-start | bytes 12582920 | tf_op jit(solution)/shard_map/ppermute | solution.py:12
  231.8 2.0 copy-start.1
where the time goes:
time: 235 us; the launch traced here: 234 us
  waiting for transfers between devices  153 us (65%)
  local copies, waits for them, and re-layouts  37.3 us (16%)
  starting transfers between devices  15.5 us (7%)
  matrix products  10.4 us (4%)
  other arithmetic  9.74 us (4%)
  between operations  7.71 us (3%)
    ppermute x4, waiting for transfers between devices, shifted(): return lax.ppermute(shard, axis, pairs)  153 us
    ppermute x4, starting transfers between devices, shifted(): return lax.ppermute(shard, axis, pairs)  15.5 us
    dynamic_update_slice x2, local copies, waits for them, and re-layouts, local(): lax.dynamic_update_slice(buffer, current + grads[:, which_pos], corner)  13.3 us
    another operation x7, local copies, waits for them, and re-layouts  6.08 us
    dot_general x8, matrix products, left_mult(): jnp.einsum('ab,nmbc->nmac', table, values, preferred_element_type=jnp.flo...  5.25 us
    dot_general x8, matrix products, right_mult(): jnp.einsum('nmab,bc->nmac', values, table, preferred_element_type=jnp.flo...  5.13 us
  transfers between devices with their start and end apart: 4, of which 4 were waited for; matrix products, arithmetic and copies ran while one was open for 2% of the time, Pallas kernels for 0%

commit v1 on v0

v1 whole, which is shorter than its diff:
```python
import functools
import math
import numpy as np
import jax, jax.numpy as jnp
from jax import lax
from jax.experimental import pallas as pl
from jax.experimental.pallas import tpu as pltpu
from jax.sharding import PartitionSpec as PS
BF=jnp.bfloat16; F32=jnp.float32
N=256; HF=128
MODES=4

def tables():
    k=np.arange(N); ph=(k[:,None]*k[None,:])%N
    ang=ph*(2*math.pi/N)
    fr=np.cos(ang)/16.0; fi=-np.sin(ang)/16.0
    tb=np.concatenate([fr[0::2],fi[0::2],fr[1::2],fi[1::2]],0)
    return jnp.asarray(tb,dtype=BF), jnp.asarray(tb.T,dtype=BF)

def dot(a,b): return jnp.dot(a,b,preferred_element_type=F32)
def iota(shape,d): return lax.broadcasted_iota(jnp.int32,shape,d)

def prep_tables(tb,tbt,tab,y,c):
    for r,f1,f2 in ((y,0,1),(c,3,2)):
        onehot=(iota((N,HF),0)==((iota((N,HF),1)-r)&255)).astype(F32).astype(BF)
        m1=dot(tb[...],onehot).astype(BF)
        onet=(iota((HF,N),1)==((iota((HF,N),0)-r)&255)).astype(F32).astype(BF)
        m2=dot(onet,tbt[...]).astype(BF)
        for par in range(2):
            a=m1[par*256:par*256+128]; b=m1[par*256+128:par*256+256]
            tab[f1,par,0:128,0:128]=a; tab[f1,par,0:128,128:256]=-b
            tab[f1,par,128:256,0:128]=b; tab[f1,par,128:256,128:256]=a
            a=m2[:,par*256:par*256+128]; b=m2[:,par*256+128:par*256+256]
            tab[f2,par,0:128,0:128]=a; tab[f2,par,0:128,128:256]=b
            tab[f2,par,128:256,0:128]=-b; tab[f2,par,128:256,128:256]=a

def prep_probe(probe,pr,tmp,y,c):
    ryt=(iota((N,N),1)==((iota((N,N),0)-y)&255)).astype(F32).astype(BF)
    rc=(iota((N,N),0)==((iota((N,N),1)-c)&255)).astype(F32).astype(BF)
    for m in range(4):
        for q in range(2):
            t=dot(ryt,probe[m,q]).astype(BF)
            pr[m,q]=dot(t,rc).astype(BF)

def perms():
    i0=iota((N,N),0); i1=iota((N,N),1)
    pt=(i1==(2*(i0&127)+(i0>>7))).astype(F32).astype(BF)
    p=(i0==(2*(i1&127)+(i1>>7))).astype(F32).astype(BF)
    return pt,p

def prep_k(phase,kk):
    pt,p=perms()
    x=phase[...]
    acc=None
    for _ in range(3):
        h=x.astype(BF)
        x=x-h.astype(F32)
        t=dot(dot(pt,h).astype(BF),p)
        acc=t if acc is None else acc+t
    kk[0]=jnp.cos(acc); kk[1]=jnp.sin(acc)

def prep_meas(meas,mp):
    pt,p=perms()
    mp[...]=dot(dot(pt,meas[...]).astype(BF),p)

def s1f(tab,P,L):
    for par in range(2):
        V=dot(tab[0,par],P[par])
        for q in range(2):
            lo=V[q*128:q*128+128,:128]; hi=V[q*128:q*128+128,128:]
            L[0,par*128:par*128+128,q*128:q*128+128]=(lo+hi).astype(BF)
            L[1,par*128:par*128+128,q*128:q*128+128]=(lo-hi).astype(BF)

def s1i(tab,P,L):
    E0=dot(tab[1,0],P[0]); E1=dot(tab[1,1],P[1])
    for q in range(2):
        for cp in range(2):
            a=E0[q*128:q*128+128,cp*128:cp*128+128]; b=E1[q*128:q*128+128,cp*128:cp*128+128]
            L[cp,0:128,q*128:q*128+128]=(a+b).astype(BF)
            L[cp,128:256,q*128:q*128+128]=(a-b).astype(BF)

def s2f(tab,L,cp): return dot(L[cp],tab[2,cp])
def s2i(tab,L):
    D0=dot(L[0],tab[3,0]); D1=dot(L[1],tab[3,1])
    return [[D0[:,q*128:q*128+128]+D1[:,q*128:q*128+128], D0[:,q*128:q*128+128]-D1[:,q*128:q*128+128]] for q in range(2)]

def put_rows(P,q,uc,x):
    a=x[:128]; b=x[128:]
    P[0,q*128:q*128+128,uc*128:uc*128+128]=(a+b).astype(BF)
    P[1,q*128:q*128+128,uc*128:uc*128+128]=(a-b).astype(BF)

def put_freq(P,q,cp,x):
    P[0,q*128:q*128+128,cp*128:cp*128+128]=x[:128].astype(BF)
    P[1,q*128:q*128+128,cp*128:cp*128+128]=x[128:].astype(BF)

def phase_a(m,tab,pr,o0,kk,P,L,psi1):
    for uc in range(2):
        sl=slice(uc*128,uc*128+128)
        a=pr[m,0,:,sl].astype(F32); b=pr[m,1,:,sl].astype(F32)
        c=o0[0,:,sl].astype(F32); d=o0[1,:,sl].astype(F32)
        put_rows(P,0,uc,a*c-b*d); put_rows(P,1,uc,a*d+b*c)
    s1f(tab,P,L)
    for cp in range(2):
        S=s2f(tab,L,cp)
        sl=slice(cp*128,cp*128+128)
        kr=kk[0,:,sl]; ki=kk[1,:,sl]
        put_freq(P,0,cp,S[:,:128]*kr-S[:,128:]*ki)
        put_freq(P,1,cp,S[:,:128]*ki+S[:,128:]*kr)
    s1i(tab,P,L)
    D=s2i(tab,L)
    for uc in range(2):
        sl=slice(uc*128,uc*128+128)
        for q in range(2): psi1[m,q,:,sl]=D[q][uc]

def phase_b(m,tab,o1,P,L,psi1,far,inten):
    for uc in range(2):
        sl=slice(uc*128,uc*128+128)
        a=psi1[m,0,:,sl]; b=psi1[m,1,:,sl]
        c=o1[0,:,sl].astype(F32); d=o1[1,:,sl].astype(F32)
        put_rows(P,0,uc,a*c-b*d); put_rows(P,1,uc,a*d+b*c)
    s1f(tab,P,L)
    for cp in range(2):
        S=s2f(tab,L,cp)
        far[m,cp]=S
        inten[cp]+=S[:,:128]*S[:,:128]+S[:,128:]*S[:,128:]

def phase_c(m,tab,o1,P,L,psi1,far,inten,g1,adj):
    for cp in range(2):
        w=inten[cp]
        put_freq(P,0,cp,w*far[m,cp,:,:128]); put_freq(P,1,cp,w*far[m,cp,:,128:])
    s1i(tab,P,L)
    D=s2i(tab,L)
    for uc in range(2):
        sl=slice(uc*128,uc*128+128)
        br=D[0][uc]; bi=D[1][uc]
        a=psi1[m,0,:,sl]; b=psi1[m,1,:,sl]
        g1[0,:,sl]+=a*br+b*bi; g1[1,:,sl]+=a*bi-b*br
        c=o1[0,:,sl].astype(F32); d=o1[1,:,sl].astype(F32)
        put_rows(adj.at[m],0,uc,c*br+d*bi); put_rows(adj.at[m],1,uc,c*bi-d*br)

def phase_d(m,tab,pr,kk,P,L,adj,g0):
    s1f(tab,adj.at[m],L)
    for cp in range(2):
        S=s2f(tab,L,cp).astype(BF).astype(F32)
        sl=slice(cp*128,cp*128+128)
        kr=kk[0,:,sl]; ki=kk[1,:,sl]
        put_freq(P,0,cp,kr*S[:,:128]+ki*S[:,128:])
        put_freq(P,1,cp,kr*S[:,128:]-ki*S[:,:128])
    s1i(tab,P,L)
    D=s2i(tab,L)
    for uc in range(2):
        sl=slice(uc*128,uc*128+128)
        wr=D[0][uc]; wi=D[1][uc]
        a=pr[m,0,:,sl].astype(F32); b=pr[m,1,:,sl].astype(F32)
        g0[0,:,sl]+=a*wr+b*wi; g0[1,:,sl]+=a*wi-b*wr


MESH = pl.DeviceIdType.MESH


def main_kernel(chips, height, pos, obj, probe_h, phase_h, meas_h, tb_h, tbt_h, out,
                band, w_left, w_right, w_part, near, farw, ob, probe, phase, meas, mtmp,
                tb, tbt, tab, pr, kk, mp, P, L, psi1, far, inten, adj, g, gs,
                in_sem, obj_send, obj_recv, near_send, near_recv, m_send, m_recv,
                g_send, g_recv, loc_sem):
    d = lax.axis_index("depth")
    p = lax.axis_index("pos")
    left = lax.rem(p + chips - 1, chips)
    right = lax.rem(p + 1, chips)
    nb = lax.rem(p + 1 - 2 * d + chips, chips)
    total = 2 * chips
    mine = lax.rem(2 * p - d + total, total)
    other = lax.rem(2 * p + d - 1 + total, total)
    q_left = lax.rem(2 * p - 2 + total, total)
    q_right = 2 * p + 1

    loads = [
        pltpu.make_async_copy(obj, band, in_sem.at[0]),
        pltpu.make_async_copy(meas_h.at[d], mtmp, in_sem.at[1]),
        pltpu.make_async_copy(tb_h, tb, in_sem.at[2]),
        pltpu.make_async_copy(tbt_h, tbt, in_sem.at[3]),
        pltpu.make_async_copy(probe_h, probe, in_sem.at[4]),
        pltpu.make_async_copy(phase_h, phase, in_sem.at[5]),
    ]
    for cp in loads:
        cp.start()
    barrier = pltpu.get_barrier_semaphore()
    peers = ((1 - d, p), (0, left), (1, right), (d, nb))
    for peer in peers:
        pl.semaphore_signal(barrier, inc=1, device_id=peer, device_id_type=MESH)

    blocks = height // N
    row_id = iota((N, N), 0)

    def window(q, part):
        y = pos[q, 0]
        k = y >> 8
        k2 = jnp.minimum(k + 1, blocks - 1)
        a = band[part, k]
        b = band[part, k2]
        return jnp.where(row_id >= (y & 255), a.astype(F32), b.astype(F32)).astype(BF)

    loads[0].wait()
    for part in range(2):
        w_left[part] = window(q_left, part)
    for part in range(2):
        w_right[part] = window(q_right, part)
    for part in range(2):
        w_part[part] = window(other, part)
    pl.semaphore_wait(barrier, 4)

    def remote(src, dst, ss, rs, dev):
        return pltpu.make_async_remote_copy(src_ref=src, dst_ref=dst, send_sem=ss, recv_sem=rs,
                                            device_id=dev, device_id_type=MESH)

    c_left = remote(w_left, farw.at[d], obj_send.at[0], obj_recv.at[d], (0, left))
    c_right = remote(w_right, farw.at[d], obj_send.at[1], obj_recv.at[d], (1, right))
    c_part = remote(w_part, near.at[d], near_send, near_recv, (1 - d, p))
    c_left.start()
    c_right.start()
    c_part.start()
    for part in range(2):
        near[d, part] = window(mine, part)

    loads[1].wait()
    c_meas = remote(meas.at[0], meas.at[1], m_send, m_recv, (1, right))
    meas[0] = mtmp[...].astype(BF)

    @pl.when(d == 1)
    def _():
        c_meas.start()

    y = pos[mine, 0] & 255
    c = pos[mine, 1] & 255
    loads[2].wait()
    loads[3].wait()
    prep_tables(tb, tbt, tab, y, c)
    loads[4].wait()
    prep_probe(probe, pr, None, y, c)
    loads[5].wait()
    prep_k(phase, kk)
    inten[...] = jnp.zeros_like(inten)
    g[...] = jnp.zeros_like(g)

    near_mask = (iota((N, N), 1) - c) * (1 - 2 * d) - d >= 0

    def merge(s):
        for part in range(2):
            ob[s, part] = jnp.where(near_mask, near[s, part].astype(F32),
                                    farw[s, part].astype(F32)).astype(BF)

    def loop(f):
        for m in range(MODES):
            f(m)

    c_part.wait_recv()
    remote(w_left, farw.at[0], obj_send.at[0], obj_recv.at[0], (0, left)).wait_recv()
    merge(0)
    loop(lambda m: phase_a(m, tab, pr, ob.at[0], kk, P, L, psi1))
    remote(w_left, farw.at[1], obj_send.at[0], obj_recv.at[1], (0, left)).wait_recv()
    merge(1)
    loop(lambda m: phase_b(m, tab, ob.at[1], P, L, psi1, far, inten))

    @pl.when(d == 1)
    def _():
        c_meas.wait()

    prep_meas(meas.at[d], mp)
    for cp in range(2):
        inten[cp] = (inten[cp] - mp[:, cp * 128:cp * 128 + 128]) * 0.125
    loop(lambda m: phase_c(m, tab, ob.at[1], P, L, psi1, far, inten, g.at[1], adj))

    def ship(s):
        gs[s] = g[s].astype(BF)
        to_far = remote(gs.at[s], out.at[2 + d], g_send.at[s], g_recv.at[2 + d], (s, nb))
        to_near = remote(gs.at[s], out.at[d], g_send.at[2], g_recv.at[d], (s, p))
        stay = pltpu.make_async_copy(gs.at[s], out.at[d], loc_sem)
        to_far.start()

        @pl.when(d != s)
        def _():
            to_near.start()

        @pl.when(d == s)
        def _():
            stay.start()

        return to_far, to_near, stay

    first = ship(1)
    loop(lambda m: phase_d(m, tab, pr, kk, P, L, adj, g.at[0]))
    last = ship(0)

    c_left.wait_send()
    c_right.wait_send()
    c_part.wait_send()
    for s, (to_far, to_near, stay) in ((1, first), (0, last)):
        to_far.wait_send()

        @pl.when(d != s)
        def _():
            to_near.wait_send()

        @pl.when(d == s)
        def _():
            stay.wait()

    remote(gs.at[0], out.at[1 - d], g_send.at[2], g_recv.at[1 - d], (0, p)).wait_recv()
    remote(gs.at[0], out.at[2], g_send.at[0], g_recv.at[2], (0, nb)).wait_recv()
    remote(gs.at[0], out.at[3], g_send.at[0], g_recv.at[3], (0, nb)).wait_recv()


def final_kernel(chips, blocks, pos, slots, out):
    i = pl.program_id(0)
    p = lax.axis_index("pos")
    total = 2 * chips
    out[...] = jnp.zeros_like(out)
    rows = iota((N, N), 0)
    cols = iota((N, N), 1)
    for slot, (off, ge) in enumerate(((0, True), (total - 1, False), (total - 2, False), (1, True))):
        q = lax.rem(2 * p + off, total)
        y = pos[q, 0]
        k = y >> 8
        yy = y & 255
        c = pos[q, 1] & 255
        cm = (cols >= c) if ge else (cols < c)
        for step in range(2):

            @pl.when(i == k + step)
            def _():
                rm = (rows >= yy) if step == 0 else (rows < yy)
                for part in range(2):
                    out[part] = out[part] + jnp.where(cm & rm, slots[slot, part].astype(F32), 0.0)


def final_wrap(chips, blocks, pos, slots, out, acc):
    final_kernel(chips, blocks, pos, slots, acc)
    out[...] = acc[...].astype(BF)


def local(object_field, probe, prop_phase, measured, positions):
    chips = lax.axis_size("pos")
    height = object_field.shape[2]
    blocks = height // N
    tb, tbt = tables()
    any_ = pl.BlockSpec(memory_space=pl.ANY)
    smem = pl.BlockSpec(memory_space=pltpu.SMEM)
    V = pltpu.VMEM
    win = V((2, N, N), BF)
    dma = pltpu.SemaphoreType.DMA
    slots = pl.pallas_call(
        functools.partial(main_kernel, chips, height),
        out_shape=jax.ShapeDtypeStruct((4, 2, N, N), BF),
        in_specs=[smem] + [pl.BlockSpec(memory_space=pltpu.HBM)] * 6,
        out_specs=any_,
        scratch_shapes=[
            V((2, blocks, N, N), BF), win, win, win, V((2, 2, N, N), BF), V((2, 2, N, N), BF),
            V((2, 2, N, N), BF), V((4, 2, N, N), BF), V((N, N), F32), V((2, N, N), BF), V((N, N), F32),
            V((512, N), BF), V((N, 512), BF), V((4, 2, N, N), BF), V((4, 2, N, N), BF),
            V((2, N, N), F32), V((N, N), F32), V((2, N, N), BF), V((2, N, N), BF),
            V((4, 2, N, N), F32), V((4, 2, N, N), F32), V((2, N, 128), F32), V((4, 2, N, N), BF),
            V((2, 2, N, N), F32), V((2, 2, N, N), BF),
            dma((6,)), dma((2,)), dma((2,)), dma, dma, dma, dma, dma((3,)), dma((4,)), dma,
        ],
        compiler_params=pltpu.CompilerParams(
            collective_id=0, has_side_effects=True, vmem_limit_bytes=48 * 1024 * 1024),
        name="ptycho",
    )(positions, object_field.reshape(2, blocks, N, N), probe, prop_phase, measured, tb, tbt)
    band = pl.pallas_call(
        functools.partial(final_wrap, chips, blocks),
        out_shape=jax.ShapeDtypeStruct((2, height, N), BF),
        grid_spec=pltpu.PrefetchScalarGridSpec(
            num_scalar_prefetch=1, grid=(blocks,),
            in_specs=[pl.BlockSpec((4, 2, N, N), lambda i, s: (0, 0, 0, 0))],
            out_specs=pl.BlockSpec((2, N, N), lambda i, s: (0, i, 0)),
            scratch_shapes=[V((2, N, N), F32)]),
        compiler_params=pltpu.CompilerParams(vmem_limit_bytes=16 * 1024 * 1024),
        name="assemble",
    )(positions, slots)
    return band[None]


def solution(mesh):
    placed = (PS("depth", None, None, "pos"), PS(), PS(), PS("pos", None, None), PS())
    return jax.shard_map(
        local, mesh=mesh, in_specs=placed, out_specs=PS("depth", None, None, "pos"), check_vma=False
    )
```

time: 235 us -> 54.9 us (0.23)
  the two profiles are of different devices: /device:TPU:6 before, /device:TPU:0 now
where the time goes in v1:
time: 54.9 us; the launch traced here: 54.6 us
  Pallas kernels  47 us (86%)
  local copies, waits for them, and re-layouts  7.51 us (14%)
    pallas_call x1, Pallas kernels, local(): pl.pallas_call(functools.partial(main_kernel, chips, height), out_shape=j...  40.5 us
    unnamed x13, local copies, waits for them, and re-layouts  7.51 us
    pallas_call x1, Pallas kernels, local(): pl.pallas_call(functools.partial(final_wrap, chips, blocks), out_shape=ja...  6.57 us

profile of v1, /device:TPU:0, one launch (start us, length us, event | category | flops | bytes accessed | tf_op | source)
XLA Modules:
  0.0 54.6 jit_solution(9186677676395571238)
XLA Ops:
  0.0 0.8 %copy.9.pos = s32[256,2]{1,0:T(8,128)S(1)} copy(s32[256,2]{0,1:T(2,128)} %param.11) | data formatting | bytes 4096 | tf_op args[4]
  0.8 0.0 copy-start
  0.8 1.6 %copy-done = bf16[1,2,2048,256]{3,2,1,0:T(8,128)(2,1)S(1)} copy-done((bf16[1,2,2048,256]{3,2,1,0:T(8,128)(2,1)S(1)}, bf16[1,2,2048,256]{3,2,1,0:T(8,128)(2,1)}, u32[]{:S(2)}) %copy-start) | copy-done | bytes 2097176
  2.4 0.0 copy-start.1
  2.4 1.2 %copy-done.1 = bf16[4,2,256,256]{3,2,1,0:T(8,128)(2,1)S(1)} copy-done((bf16[4,2,256,256]{3,2,1,0:T(8,128)(2,1)S(1)}, bf16[4,2,256,256]{3,2,1,0:T(8,128)(2,1)}, u32[]{:S(2)}) %copy-start.1) | copy-done | bytes 1048600
  3.6 0.0 copy-start.2
  3.6 1.0 %copy-done.2 = f32[2,256,256]{2,1,0:T(8,128)S(1)} copy-done((f32[2,256,256]{2,1,0:T(8,128)S(1)}, f32[2,256,256]{2,1,0:T(8,128)}, u32[]{:S(2)}) %copy-start.2) | copy-done | bytes 524312
  4.7 0.0 copy-start.3
  4.7 0.9 %copy-done.3 = f32[256,256]{1,0:T(8,128)S(1)} copy-done((f32[256,256]{1,0:T(8,128)S(1)}, f32[256,256]{1,0:T(8,128)}, u32[]{:S(2)}) %copy-start.3) | copy-done | bytes 262168
  5.6 0.0 copy-start.4
  5.6 0.9 %copy-done.4 = bf16[256,512]{1,0:T(8,128)(2,1)S(1)} copy-done((bf16[256,512]{1,0:T(8,128)(2,1)S(1)}, bf16[256,512]{1,0:T(8,128)(2,1)}, u32[]{:S(2)}) %copy-start.4) | copy-done | bytes 262168
  6.6 0.0 copy-start.5
  6.6 0.9 %copy-done.5 = bf16[512,256]{1,0:T(8,128)(2,1)S(1)} copy-done((bf16[512,256]{1,0:T(8,128)(2,1)S(1)}, bf16[512,256]{1,0:T(8,128)(2,1)}, u32[]{:S(2)}) %copy-start.5) | copy-done | bytes 262168
  7.5 40.5 %ptycho.1.slots = bf16[4,2,256,256]{3,2,1,0:T(8,128)(2,1)S(1)} custom-call(s32[256,2]{1,0:T(8,128)S(1)} %copy.9.pos, bf16[2,8,256,256]{3,2,1,0:T(8,128)(2,1)S(1)} %bitcast.2, bf16[4,2,256,256]{3,2,1,0:T(8,128)(2,1)S(1)} %copy-done.1, f32[256,256]{1,0:T(8,128)S(1)} %copy-done.3, f32[2,256,256]{2,1,0:T(8,128)S(1)} %copy-done.2, ...), custom_call_target="tpu_custom_call" | custom-call | tf_op jit(solution)/shard_map/ptycho/pallas_call | solution.py:351
  48.0 6.6 %assemble.1 = bf16[2,2048,256]{2,1,0:T(8,128)(2,1)} custom-call(s32[256,2]{1,0:T(8,128)S(1)} %copy.9.pos, bf16[4,2,256,256]{3,2,1,0:T(8,128)(2,1)S(1)} %ptycho.1.slots), custom_call_target="tpu_custom_call" | custom-call | tf_op jit(solution)/shard_map/assemble/pallas_call | solution.py:369
Async XLA Ops:
  0.8 1.6 %copy-start = (bf16[1,2,2048,256]{3,2,1,0:T(8,128)(2,1)S(1)}, bf16[1,2,2048,256]{3,2,1,0:T(8,128)(2,1)}, u32[]{:S(2)}) copy-start(bf16[1,2,2048,256]{3,2,1,0:T(8,128)(2,1)} %param.7) | copy-start | bytes 6291460
  2.4 1.2 %copy-start.1 = (bf16[4,2,256,256]{3,2,1,0:T(8,128)(2,1)S(1)}, bf16[4,2,256,256]{3,2,1,0:T(8,128)(2,1)}, u32[]{:S(2)}) copy-start(bf16[4,2,256,256]{3,2,1,0:T(8,128)(2,1)} %probe_h.1) | copy-start | bytes 3145732
  3.6 1.0 %copy-start.2 = (f32[2,256,256]{2,1,0:T(8,128)S(1)}, f32[2,256,256]{2,1,0:T(8,128)}, u32[]{:S(2)}) copy-start(f32[2,256,256]{2,1,0:T(8,128)} %meas_h.1) | copy-start | bytes 1572868
  4.7 0.9 %copy-start.3 = (f32[256,256]{1,0:T(8,128)S(1)}, f32[256,256]{1,0:T(8,128)}, u32[]{:S(2)}) copy-start(f32[256,256]{1,0:T(8,128)} %phase_h.1) | copy-start | bytes 786436
  5.6 0.9 %copy-start.4 = (bf16[256,512]{1,0:T(8,128)(2,1)S(1)}, bf16[256,512]{1,0:T(8,128)(2,1)}, u32[]{:S(2)}) copy-start(bf16[256,512]{1,0:T(8,128)(2,1)} %constant.5.clone.tbt_h) | copy-start | bytes 786436
  6.6 0.9 %copy-start.5 = (bf16[512,256]{1,0:T(8,128)(2,1)S(1)}, bf16[512,256]{1,0:T(8,128)(2,1)}, u32[]{:S(2)}) copy-start(bf16[512,256]{1,0:T(8,128)(2,1)} %constant.4.clone.tb_h) | copy-start | bytes 786436

commit v2 on v1

--- a/solution.py
+++ b/solution.py
@@ -138,7 +138,7 @@
         c=o1[0,:,sl].astype(F32); d=o1[1,:,sl].astype(F32)
         put_rows(adj.at[m],0,uc,c*br+d*bi); put_rows(adj.at[m],1,uc,c*bi-d*br)
 
-def phase_d(m,tab,pr,kk,P,L,adj,g0):
+def phase_d(m,tab,kk,P,L,L2,adj):
     s1f(tab,adj.at[m],L)
     for cp in range(2):
         S=s2f(tab,L,cp).astype(BF).astype(F32)
@@ -146,23 +146,37 @@
         kr=kk[0,:,sl]; ki=kk[1,:,sl]
         put_freq(P,0,cp,kr*S[:,:128]+ki*S[:,128:])
         put_freq(P,1,cp,kr*S[:,128:]-ki*S[:,:128])
-    s1i(tab,P,L)
-    D=s2i(tab,L)
+    E0=dot(tab[1,0],P[0]); E1=dot(tab[1,1],P[1])
+    for q in range(2):
+        for cp in range(2):
+            for h in range(2):
+                r=slice(q*128+h*64,q*128+h*64+64); sl=slice(cp*128,cp*128+128); to=slice(q*128,q*128+128)
+                L2[cp,h,m,:,to]=(E0[r,sl]+E1[r,sl]).astype(BF)
+                L2[cp,2+h,m,:,to]=(E0[r,sl]-E1[r,sl]).astype(BF)
+
+def phase_e(r,tab,pr,L2,gs):
+    D0=dot(L2[0,r].reshape(256,256),tab[3,0]); D1=dot(L2[1,r].reshape(256,256),tab[3,1])
+    rows=slice(r*64,r*64+64)
     for uc in range(2):
         sl=slice(uc*128,uc*128+128)
-        wr=D[0][uc]; wi=D[1][uc]
-        a=pr[m,0,:,sl].astype(F32); b=pr[m,1,:,sl].astype(F32)
-        g0[0,:,sl]+=a*wr+b*wi; g0[1,:,sl]+=a*wi-b*wr
+        W=[D0[:,q*128:q*128+128]+D1[:,q*128:q*128+128] if uc==0 else D0[:,q*128:q*128+128]-D1[:,q*128:q*128+128] for q in range(2)]
+        gr=None
+        for m in range(4):
+            wr=W[0][m*64:m*64+64]; wi=W[1][m*64:m*64+64]
+            a=pr[m,0,rows,sl].astype(F32); b=pr[m,1,rows,sl].astype(F32)
+            tr=a*wr+b*wi; ti=a*wi-b*wr
+            gr,gi=(tr,ti) if gr is None else (gr+tr,gi+ti)
+        gs[0,rows,sl]=gr.astype(BF); gs[1,rows,sl]=gi.astype(BF)
 
 
 MESH = pl.DeviceIdType.MESH
 
 
-def main_kernel(chips, height, pos, obj, probe_h, phase_h, meas_h, tb_h, tbt_h, out,
-                band, w_left, w_right, w_part, near, farw, ob, probe, phase, meas, mtmp,
-                tb, tbt, tab, pr, kk, mp, P, L, psi1, far, inten, adj, g, gs,
+def main_kernel(chips, height, pos_h, obj, probe_h, phase_h, meas_h, tb_h, tbt_h, out,
+                pos, band, w_left, w_right, w_part, near, farw, ob, probe, phase, meas, mtmp,
+                tb, tbt, tab, pr, kk, mp, P, L, psi1, far, inten, adj, L2, g, gs,
                 in_sem, obj_send, obj_recv, near_send, near_recv, m_send, m_recv,
-                g_send, g_recv, loc_sem):
+                g_send, g_recv, c_send, c_recv, loc_sem):
     d = lax.axis_index("depth")
     p = lax.axis_index("pos")
     left = lax.rem(p + chips - 1, chips)
@@ -181,6 +195,7 @@
         pltpu.make_async_copy(tbt_h, tbt, in_sem.at[3]),
         pltpu.make_async_copy(probe_h, probe, in_sem.at[4]),
         pltpu.make_async_copy(phase_h, phase, in_sem.at[5]),
+        pltpu.make_async_copy(pos_h, pos, in_sem.at[6]),
     ]
     for cp in loads:
         cp.start()
@@ -193,13 +208,14 @@
     row_id = iota((N, N), 0)
 
     def window(q, part):
-        y = pos[q, 0]
+        y = pos[0, q]
         k = y >> 8
         k2 = jnp.minimum(k + 1, blocks - 1)
         a = band[part, k]
         b = band[part, k2]
         return jnp.where(row_id >= (y & 255), a.astype(F32), b.astype(F32)).astype(BF)
 
+    loads[6].wait()
     loads[0].wait()
     for part in range(2):
         w_left[part] = window(q_left, part)
@@ -216,9 +232,13 @@
     c_left = remote(w_left, farw.at[d], obj_send.at[0], obj_recv.at[d], (0, left))
     c_right = remote(w_right, farw.at[d], obj_send.at[1], obj_recv.at[d], (1, right))
     c_part = remote(w_part, near.at[d], near_send, near_recv, (1 - d, p))
-    c_left.start()
-    c_right.start()
     c_part.start()
+
+    @pl.when(d == 0)
+    def _():
+        c_left.start()
+        c_right.start()
+
     for part in range(2):
         near[d, part] = window(mine, part)
 
@@ -226,17 +246,19 @@
     c_meas = remote(meas.at[0], meas.at[1], m_send, m_recv, (1, right))
     meas[0] = mtmp[...].astype(BF)
 
-    @pl.when(d == 1)
-    def _():
-        c_meas.start()
-
-    y = pos[mine, 0] & 255
-    c = pos[mine, 1] & 255
+    y = pos[0, mine] & 255
+    c = pos[1, mine] & 255
     loads[2].wait()
     loads[3].wait()
     prep_tables(tb, tbt, tab, y, c)
     loads[4].wait()
     prep_probe(probe, pr, None, y, c)
+    @pl.when(d == 1)
+    def _():
+        c_left.start()
+        c_right.start()
+        c_meas.start()
+
     loads[5].wait()
     prep_k(phase, kk)
     inten[...] = jnp.zeros_like(inten)
@@ -268,74 +290,101 @@
     prep_meas(meas.at[d], mp)
     for cp in range(2):
         inten[cp] = (inten[cp] - mp[:, cp * 128:cp * 128 + 128]) * 0.125
-    loop(lambda m: phase_c(m, tab, ob.at[1], P, L, psi1, far, inten, g.at[1], adj))
-
-    def ship(s):
-        gs[s] = g[s].astype(BF)
-        to_far = remote(gs.at[s], out.at[2 + d], g_send.at[s], g_recv.at[2 + d], (s, nb))
-        to_near = remote(gs.at[s], out.at[d], g_send.at[2], g_recv.at[d], (s, p))
-        stay = pltpu.make_async_copy(gs.at[s], out.at[d], loc_sem)
-        to_far.start()
-
-        @pl.when(d != s)
-        def _():
-            to_near.start()
-
-        @pl.when(d == s)
-        def _():
-            stay.start()
-
-        return to_far, to_near, stay
-
-    first = ship(1)
-    loop(lambda m: phase_d(m, tab, pr, kk, P, L, adj, g.at[0]))
-    last = ship(0)
+    loop(lambda m: phase_c(m, tab, ob.at[1], P, L, psi1, far, inten, g, adj))
+
+    gs[1] = g[...].astype(BF)
+    far1 = remote(gs.at[1], out.at[2 + d], g_send.at[0], g_recv.at[2 + d], (1, nb))
+    near1 = remote(gs.at[1], out.at[d], g_send.at[1], g_recv.at[d], (1, p))
+    stay1 = pltpu.make_async_copy(gs.at[1], out.at[d], loc_sem)
+    far1.start()
+
+    @pl.when(d == 0)
+    def _():
+        near1.start()
+
+    @pl.when(d == 1)
+    def _():
+        stay1.start()
+
+    loop(lambda m: phase_d(m, tab, kk, P, L, L2, adj))
+
+    def chunk(r, dev):
+        rows = pl.ds(r * 64, 64)
+        return remote(gs.at[0, :, rows, :], out.at[2 + d, :, rows, :], c_send.at[r], c_recv.at[d, r], dev)
+
+    def incoming(slot, r):
+        rows = pl.ds(r * 64, 64)
+        return remote(gs.at[0, :, rows, :], out.at[2 + slot, :, rows, :], c_send.at[r], c_recv.at[slot, r],
+                      (0, nb))
+
+    for r in range(4):
+        phase_e(r, tab, pr, L2, gs.at[0])
+        chunk(r, (0, nb)).start()
+    near0 = remote(gs.at[0], out.at[d], g_send.at[1], g_recv.at[d], (0, p))
+    stay0 = pltpu.make_async_copy(gs.at[0], out.at[d], loc_sem)
+
+    @pl.when(d == 1)
+    def _():
+        near0.start()
+        stay1.wait()
+
+    @pl.when(d == 0)
+    def _():
+        stay0.start()
+        near1.wait_send()
 
     c_left.wait_send()
     c_right.wait_send()
     c_part.wait_send()
-    for s, (to_far, to_near, stay) in ((1, first), (0, last)):
-        to_far.wait_send()
-
-        @pl.when(d != s)
-        def _():
-            to_near.wait_send()
-
-        @pl.when(d == s)
-        def _():
-            stay.wait()
-
-    remote(gs.at[0], out.at[1 - d], g_send.at[2], g_recv.at[1 - d], (0, p)).wait_recv()
-    remote(gs.at[0], out.at[2], g_send.at[0], g_recv.at[2], (0, nb)).wait_recv()
-    remote(gs.at[0], out.at[3], g_send.at[0], g_recv.at[3], (0, nb)).wait_recv()
-
-
-def final_kernel(chips, blocks, pos, slots, out):
-    i = pl.program_id(0)
+    far1.wait_send()
+    for r in range(4):
+        chunk(r, (0, nb)).wait_send()
+
+    @pl.when(d == 1)
+    def _():
+        near0.wait_send()
+        remote(gs.at[1], out.at[0], g_send.at[1], g_recv.at[0], (0, p)).wait_recv()
+        for k in range(2):
+            remote(gs.at[1], out.at[2 + k], g_send.at[0], g_recv.at[2 + k], (1, nb)).wait_recv()
+
+    @pl.when(d == 0)
+    def _():
+        stay0.wait()
+        remote(gs.at[0], out.at[1], g_send.at[1], g_recv.at[1], (0, p)).wait_recv()
+        for k in range(2):
+            for r in range(4):
+                incoming(k, r).wait_recv()
+
+
+def final_kernel(chips, blocks, pos_h, slots, out, pos, acc, ob, sem, pos_sem):
+    load = pltpu.make_async_copy(pos_h, pos, pos_sem)
+    load.start()
     p = lax.axis_index("pos")
     total = 2 * chips
-    out[...] = jnp.zeros_like(out)
+    acc[...] = jnp.zeros_like(acc)
+    load.wait()
     rows = iota((N, N), 0)
     cols = iota((N, N), 1)
     for slot, (off, ge) in enumerate(((0, True), (total - 1, False), (total - 2, False), (1, True))):
         q = lax.rem(2 * p + off, total)
-        y = pos[q, 0]
+        y = pos[0, q]
         k = y >> 8
+        k2 = jnp.minimum(k + 1, blocks - 1)
         yy = y & 255
-        c = pos[q, 1] & 255
+        c = pos[1, q] & 255
         cm = (cols >= c) if ge else (cols < c)
-        for step in range(2):
-
-            @pl.when(i == k + step)
-            def _():
-                rm = (rows >= yy) if step == 0 else (rows < yy)
-                for part in range(2):
-                    out[part] = out[part] + jnp.where(cm & rm, slots[slot, part].astype(F32), 0.0)
-
-
-def final_wrap(chips, blocks, pos, slots, out, acc):
-    final_kernel(chips, blocks, pos, slots, acc)
-    out[...] = acc[...].astype(BF)
+        for part in range(2):
+            x = slots[slot, part].astype(F32)
+            acc[part, k] += jnp.where(cm & (rows >= yy), x, 0.0)
+            acc[part, k2] += jnp.where(cm & (rows < yy), x, 0.0)
+    copies = []
+    for i in range(blocks):
+        ob[:, i] = acc[:, i].astype(BF)
+        cp = pltpu.make_async_copy(ob.at[:, i], out.at[:, i], sem.at[i])
+        cp.start()
+        copies.append(cp)
+    for cp in copies:
+        cp.wait()
 
 
 def local(object_field, probe, prop_phase, measured, positions):
@@ -343,41 +392,41 @@
     height = object_field.shape[2]
     blocks = height // N
     tb, tbt = tables()
+    pos_t = positions.T
     any_ = pl.BlockSpec(memory_space=pl.ANY)
-    smem = pl.BlockSpec(memory_space=pltpu.SMEM)
     V = pltpu.VMEM
     win = V((2, N, N), BF)
     dma = pltpu.SemaphoreType.DMA
     slots = pl.pallas_call(
         functools.partial(main_kernel, chips, height),
         out_shape=jax.ShapeDtypeStruct((4, 2, N, N), BF),
-        in_specs=[smem] + [pl.BlockSpec(memory_space=pltpu.HBM)] * 6,
+        in_specs=[pl.BlockSpec(memory_space=pltpu.HBM)] * 7,
         out_specs=any_,
         scratch_shapes=[
-            V((2, blocks, N, N), BF), win, win, win, V((2, 2, N, N), BF), V((2, 2, N, N), BF),
+            pltpu.SMEM((2, 2 * chips), jnp.int32), V((2, blocks, N, N), BF), win, win, win, V((2, 2, N, N), BF), V((2, 2, N, N), BF),
             V((2, 2, N, N), BF), V((4, 2, N, N), BF), V((N, N), F32), V((2, N, N), BF), V((N, N), F32),
             V((512, N), BF), V((N, 512), BF), V((4, 2, N, N), BF), V((4, 2, N, N), BF),
             V((2, N, N), F32), V((N, N), F32), V((2, N, N), BF), V((2, N, N), BF),
             V((4, 2, N, N), F32), V((4, 2, N, N), F32), V((2, N, 128), F32), V((4, 2, N, N), BF),
-            V((2, 2, N, N), F32), V((2, 2, N, N), BF),
-            dma((6,)), dma((2,)), dma((2,)), dma, dma, dma, dma, dma((3,)), dma((4,)), dma,
+            V((2, 4, 4, 64, N), BF), V((2, N, N), F32), V((2, 2, N, N), BF),
+            dma((7,)), dma((2,)), dma((2,)), dma, dma, dma, dma, dma((2,)), dma((4,)), dma((4,)), dma((2, 4)), dma,
         ],
         compiler_params=pltpu.CompilerParams(
             collective_id=0, has_side_effects=True, vmem_limit_bytes=48 * 1024 * 1024),
         name="ptycho",
-    )(positions, object_field.reshape(2, blocks, N, N), probe, prop_phase, measured, tb, tbt)
+    )(*(pltpu.with_memory_space_constraint(a, pltpu.HBM) for a in (
+        pos_t, object_field.reshape(2, blocks, N, N), probe, prop_phase, measured, tb, tbt)))
     band = pl.pallas_call(
-        functools.partial(final_wrap, chips, blocks),
-        out_shape=jax.ShapeDtypeStruct((2, height, N), BF),
-        grid_spec=pltpu.PrefetchScalarGridSpec(
-            num_scalar_prefetch=1, grid=(blocks,),
-            in_specs=[pl.BlockSpec((4, 2, N, N), lambda i, s: (0, 0, 0, 0))],
-            out_specs=pl.BlockSpec((2, N, N), lambda i, s: (0, i, 0)),
-            scratch_shapes=[V((2, N, N), F32)]),
-        compiler_params=pltpu.CompilerParams(vmem_limit_bytes=16 * 1024 * 1024),
+        functools.partial(final_kernel, chips, blocks),
+        out_shape=jax.ShapeDtypeStruct((2, blocks, N, N), BF),
+        in_specs=[pl.BlockSpec(memory_space=pltpu.HBM), pl.BlockSpec(memory_space=pltpu.VMEM)],
+        out_specs=pl.BlockSpec(memory_space=pltpu.HBM),
+        scratch_shapes=[pltpu.SMEM((2, 2 * chips), jnp.int32), V((2, blocks, N, N), F32), V((2, blocks, N, N), BF),
+                        dma((blocks,)), dma],
+        compiler_params=pltpu.CompilerParams(vmem_limit_bytes=32 * 1024 * 1024),
         name="assemble",
-    )(positions, slots)
-    return band[None]
+    )(pltpu.with_memory_space_constraint(pos_t, pltpu.HBM), slots)
+    return band.reshape(1, 2, height, N)
 
 
 def solution(mesh):

time: 54.9 us -> 40.2 us (0.73)
  local copies, waits for them, and re-layouts: 7.51 us -> 0 us
  Pallas kernels: 47 us -> 40.1 us
    unnamed x13 -> x0, local copies, waits for them, and re-layouts: 7.51 us -> none
    pallas_call x1, Pallas kernels: 6.57 us -> 2.88 us  [local(): pl.pallas_call(functools.partial(final_kernel, chips, blocks), out_shape=...]
    pallas_call x1, Pallas kernels: 40.5 us -> 37.2 us  [local(): pl.pallas_call(functools.partial(main_kernel, chips, height), out_shape=j...]
where the time goes in v2:
time: 40.2 us; the launch traced here: 40.1 us
  Pallas kernels  40.1 us (100%)
    pallas_call x1, Pallas kernels, local(): pl.pallas_call(functools.partial(main_kernel, chips, height), out_shape=j...  37.2 us
    pallas_call x1, Pallas kernels, local(): pl.pallas_call(functools.partial(final_kernel, chips, blocks), out_shape=...  2.88 us

profile of v2, /device:TPU:0, one launch (start us, length us, event | category | flops | bytes accessed | tf_op | source)
XLA Modules:
  0.0 40.1 jit_solution(9125354106875442601)
XLA Ops:
  0.0 37.2 %ptycho.1.slots = bf16[4,2,256,256]{3,2,1,0:T(8,128)(2,1)S(1)} custom-call(s32[2,256]{1,0:T(2,128)} %bitcast.4, bf16[2,8,256,256]{3,2,1,0:T(8,128)(2,1)} %bitcast.3, bf16[4,2,256,256]{3,2,1,0:T(8,128)(2,1)} %probe_h.1, f32[256,256]{1,0:T(8,128)} %phase_h.1, f32[2,256,256]{2,1,0:T(8,128)} %meas_h.1, bf16[512,256]{1,0:T(8,128)(2,1)} %constant.4.clone.tb_h, ...), custom_call_target="tpu_custom_call" | custom-call | tf_op jit(solution)/shard_map/ptycho/pallas_call | solution.py:400
  37.2 2.9 %assemble.1 = bf16[2,8,256,256]{3,2,1,0:T(8,128)(2,1)} custom-call(s32[2,256]{1,0:T(2,128)} %bitcast.5, bf16[4,2,256,256]{3,2,1,0:T(8,128)(2,1)S(1)} %ptycho.1.slots), custom_call_target="tpu_custom_call" | custom-call | tf_op jit(solution)/shard_map/assemble/pallas_call | solution.py:419

commit v3 on v2

--- a/solution.py
+++ b/solution.py
@@ -176,7 +176,7 @@
                 pos, band, w_left, w_right, w_part, near, farw, ob, probe, phase, meas, mtmp,
                 tb, tbt, tab, pr, kk, mp, P, L, psi1, far, inten, adj, L2, g, gs,
                 in_sem, obj_send, obj_recv, near_send, near_recv, m_send, m_recv,
-                g_send, g_recv, c_send, c_recv, loc_sem):
+                g_send, g_recv, c_send, c_recv, loc_sem, turn):
     d = lax.axis_index("depth")
     p = lax.axis_index("pos")
     left = lax.rem(p + chips - 1, chips)
@@ -223,29 +223,8 @@
         w_right[part] = window(q_right, part)
     for part in range(2):
         w_part[part] = window(other, part)
-    pl.semaphore_wait(barrier, 4)
-
-    def remote(src, dst, ss, rs, dev):
-        return pltpu.make_async_remote_copy(src_ref=src, dst_ref=dst, send_sem=ss, recv_sem=rs,
-                                            device_id=dev, device_id_type=MESH)
-
-    c_left = remote(w_left, farw.at[d], obj_send.at[0], obj_recv.at[d], (0, left))
-    c_right = remote(w_right, farw.at[d], obj_send.at[1], obj_recv.at[d], (1, right))
-    c_part = remote(w_part, near.at[d], near_send, near_recv, (1 - d, p))
-    c_part.start()
-
-    @pl.when(d == 0)
-    def _():
-        c_left.start()
-        c_right.start()
-
     for part in range(2):
         near[d, part] = window(mine, part)
-
-    loads[1].wait()
-    c_meas = remote(meas.at[0], meas.at[1], m_send, m_recv, (1, right))
-    meas[0] = mtmp[...].astype(BF)
-
     y = pos[0, mine] & 255
     c = pos[1, mine] & 255
     loads[2].wait()
@@ -253,14 +232,54 @@
     prep_tables(tb, tbt, tab, y, c)
     loads[4].wait()
     prep_probe(probe, pr, None, y, c)
-    @pl.when(d == 1)
-    def _():
-        c_left.start()
+    pl.semaphore_wait(barrier, 4)
+
+    def remote(src, dst, ss, rs, dev):
+        return pltpu.make_async_remote_copy(src_ref=src, dst_ref=dst, send_sem=ss, recv_sem=rs,
+                                            device_id=dev, device_id_type=MESH)
+
+    c_left = remote(w_left, farw.at[d], obj_send.at[0], obj_recv.at[d], (0, left))
+    c_right = remote(w_right, farw.at[d], obj_send.at[1], obj_recv.at[d], (1, right))
+    c_part = remote(w_part, near.at[d], near_send, near_recv, (1 - d, p))
+    go_left = p > 0
+    wrap_a = jnp.logical_and(d == 0, p == chips - 1)
+
+    def send_object():
+        @pl.when(go_left)
+        def _():
+            c_left.start()
+
         c_right.start()
-        c_meas.start()
-
+
+    def sent_object():
+        @pl.when(go_left)
+        def _():
+            c_left.wait_send()
+
+        c_right.wait_send()
+
+    @pl.when(d == 0)
+    def _():
+        send_object()
+
+    c_part.start()
+    loads[1].wait()
+    c_meas = remote(meas.at[0], meas.at[1], m_send, m_recv, (1, right))
+    meas[0] = mtmp[...].astype(BF)
     loads[5].wait()
     prep_k(phase, kk)
+
+    @pl.when(d == 0)
+    def _():
+        sent_object()
+        pl.semaphore_signal(turn, inc=1, device_id=(1, p), device_id_type=MESH)
+
+    @pl.when(d == 1)
+    def _():
+        pl.semaphore_wait(turn, 1)
+        send_object()
+        c_meas.start()
+
     inten[...] = jnp.zeros_like(inten)
     g[...] = jnp.zeros_like(g)
 
@@ -276,10 +295,16 @@
             f(m)
 
     c_part.wait_recv()
-    remote(w_left, farw.at[0], obj_send.at[0], obj_recv.at[0], (0, left)).wait_recv()
+
+    def got_far(k):
+        @pl.when(jnp.logical_not(wrap_a))
+        def _():
+            remote(w_left, farw.at[k], obj_send.at[0], obj_recv.at[k], (0, left)).wait_recv()
+
+    got_far(0)
     merge(0)
     loop(lambda m: phase_a(m, tab, pr, ob.at[0], kk, P, L, psi1))
-    remote(w_left, farw.at[1], obj_send.at[0], obj_recv.at[1], (0, left)).wait_recv()
+    got_far(1)
     merge(1)
     loop(lambda m: phase_b(m, tab, ob.at[1], P, L, psi1, far, inten))
 
@@ -296,7 +321,10 @@
     far1 = remote(gs.at[1], out.at[2 + d], g_send.at[0], g_recv.at[2 + d], (1, nb))
     near1 = remote(gs.at[1], out.at[d], g_send.at[1], g_recv.at[d], (1, p))
     stay1 = pltpu.make_async_copy(gs.at[1], out.at[d], loc_sem)
-    far1.start()
+
+    @pl.when(jnp.logical_not(wrap_a))
+    def _():
+        far1.start()
 
     @pl.when(d == 0)
     def _():
@@ -319,7 +347,11 @@
 
     for r in range(4):
         phase_e(r, tab, pr, L2, gs.at[0])
-        chunk(r, (0, nb)).start()
+
+        @pl.when(jnp.logical_not(wrap_a))
+        def _():
+            chunk(r, (0, nb)).start()
+
     near0 = remote(gs.at[0], out.at[d], g_send.at[1], g_recv.at[d], (0, p))
     stay0 = pltpu.make_async_copy(gs.at[0], out.at[d], loc_sem)
 
@@ -333,27 +365,39 @@
         stay0.start()
         near1.wait_send()
 
-    c_left.wait_send()
-    c_right.wait_send()
+    @pl.when(d == 1)
+    def _():
+        sent_object()
+
     c_part.wait_send()
-    far1.wait_send()
-    for r in range(4):
-        chunk(r, (0, nb)).wait_send()
+
+    @pl.when(jnp.logical_not(wrap_a))
+    def _():
+        far1.wait_send()
+        for r in range(4):
+            chunk(r, (0, nb)).wait_send()
 
     @pl.when(d == 1)
     def _():
         near0.wait_send()
         remote(gs.at[1], out.at[0], g_send.at[1], g_recv.at[0], (0, p)).wait_recv()
-        for k in range(2):
-            remote(gs.at[1], out.at[2 + k], g_send.at[0], g_recv.at[2 + k], (1, nb)).wait_recv()
+        remote(gs.at[1], out.at[3], g_send.at[0], g_recv.at[3], (1, nb)).wait_recv()
+
+        @pl.when(p > 0)
+        def _():
+            remote(gs.at[1], out.at[2], g_send.at[0], g_recv.at[2], (1, nb)).wait_recv()
 
     @pl.when(d == 0)
     def _():
         stay0.wait()
         remote(gs.at[0], out.at[1], g_send.at[1], g_recv.at[1], (0, p)).wait_recv()
-        for k in range(2):
+        for r in range(4):
+            incoming(1, r).wait_recv()
+
+        @pl.when(p > 0)
+        def _():
             for r in range(4):
-                incoming(k, r).wait_recv()
+                incoming(0, r).wait_recv()
 
 
 def final_kernel(chips, blocks, pos_h, slots, out, pos, acc, ob, sem, pos_sem):
@@ -409,7 +453,7 @@
             V((2, N, N), F32), V((N, N), F32), V((2, N, N), BF), V((2, N, N), BF),
             V((4, 2, N, N), F32), V((4, 2, N, N), F32), V((2, N, 128), F32), V((4, 2, N, N), BF),
             V((2, 4, 4, 64, N), BF), V((2, N, N), F32), V((2, 2, N, N), BF),
-            dma((7,)), dma((2,)), dma((2,)), dma, dma, dma, dma, dma((2,)), dma((4,)), dma((4,)), dma((2, 4)), dma,
+            dma((7,)), dma((2,)), dma((2,)), dma, dma, dma, dma, dma((2,)), dma((4,)), dma((4,)), dma((2, 4)), dma, pltpu.SemaphoreType.REGULAR,
         ],
         compiler_params=pltpu.CompilerParams(
             collective_id=0, has_side_effects=True, vmem_limit_bytes=48 * 1024 * 1024),

time: 40.2 us -> 37.1 us (0.923)
  the two profiles are of different devices: /device:TPU:0 before, /device:TPU:6 now
where the time goes in v3:
time: 37.1 us; the launch traced here: 37 us
  Pallas kernels  37 us (100%)
    pallas_call x1, Pallas kernels, local(): pl.pallas_call(functools.partial(main_kernel, chips, height), out_shape=j...  34.1 us
    pallas_call x1, Pallas kernels, local(): pl.pallas_call(functools.partial(final_kernel, chips, blocks), out_shape=...  2.88 us

profile of v3, /device:TPU:6, one launch (start us, length us, event | category | flops | bytes accessed | tf_op | source)
XLA Modules:
  0.0 37.0 jit_solution(9395026486103098645)
XLA Ops:
  0.0 34.1 %ptycho.1.slots = bf16[4,2,256,256]{3,2,1,0:T(8,128)(2,1)S(1)} custom-call(s32[2,256]{1,0:T(2,128)} %bitcast.4, bf16[2,8,256,256]{3,2,1,0:T(8,128)(2,1)} %bitcast.3, bf16[4,2,256,256]{3,2,1,0:T(8,128)(2,1)} %probe_h.1, f32[256,256]{1,0:T(8,128)} %phase_h.1, f32[2,256,256]{2,1,0:T(8,128)} %meas_h.1, bf16[512,256]{1,0:T(8,128)(2,1)} %constant.4.clone.tb_h, ...), custom_call_target="tpu_custom_call" | custom-call | tf_op jit(solution)/shard_map/ptycho/pallas_call | solution.py:444
  34.1 2.9 %assemble.1 = bf16[2,8,256,256]{3,2,1,0:T(8,128)(2,1)} custom-call(s32[2,256]{1,0:T(2,128)} %bitcast.5, bf16[4,2,256,256]{3,2,1,0:T(8,128)(2,1)S(1)} %ptycho.1.slots), custom_call_target="tpu_custom_call" | custom-call | tf_op jit(solution)/shard_map/assemble/pallas_call | solution.py:463

commit v4 on v3

--- a/solution.py
+++ b/solution.py
@@ -9,6 +9,7 @@
 BF=jnp.bfloat16; F32=jnp.float32
 N=256; HF=128
 MODES=4
+WIDTH=4
 
 def tables():
     k=np.arange(N); ph=(k[:,None]*k[None,:])%N
@@ -40,7 +41,7 @@
     for m in range(4):
         for q in range(2):
             t=dot(ryt,probe[m,q]).astype(BF)
-            pr[m,q]=dot(t,rc).astype(BF)
+            pr[m,q]=dot(t,rc)
 
 def perms():
     i0=iota((N,N),0); i1=iota((N,N),1)
@@ -63,110 +64,147 @@
     pt,p=perms()
     mp[...]=dot(dot(pt,meas[...]).astype(BF),p)
 
-def s1f(tab,P,L):
-    for par in range(2):
-        V=dot(tab[0,par],P[par])
-        for q in range(2):
-            lo=V[q*128:q*128+128,:128]; hi=V[q*128:q*128+128,128:]
-            L[0,par*128:par*128+128,q*128:q*128+128]=(lo+hi).astype(BF)
-            L[1,par*128:par*128+128,q*128:q*128+128]=(lo-hi).astype(BF)
-
-def s1i(tab,P,L):
-    E0=dot(tab[1,0],P[0]); E1=dot(tab[1,1],P[1])
+RC=32
+def dots1f(tab,P): return [dot(tab[0,par],P[par]) for par in range(2)]
+def post1f(VV,L):
     for q in range(2):
+        for r in range(0,128,RC):
+            for par in range(2):
+                V=VV[par][q*128+r:q*128+r+RC]
+                lo=V[:,:128]; hi=V[:,128:]
+                L[0,par*128+r:par*128+r+RC,q*128:q*128+128]=(lo+hi).astype(BF)
+                L[1,par*128+r:par*128+r+RC,q*128:q*128+128]=(lo-hi).astype(BF)
+
+def dots2f(tab,L): return [dot(L[cp],tab[2,cp]) for cp in range(2)]
+def dots1i(tab,P): return [dot(tab[1,par],P[par]) for par in range(2)]
+def post1i(E,L):
+    for q in range(2):
+        for r in range(0,128,RC):
+            for cp in range(2):
+                rr=slice(q*128+r,q*128+r+RC)
+                a=E[0][rr,cp*128:cp*128+128]; b=E[1][rr,cp*128:cp*128+128]
+                L[cp,r:r+RC,q*128:q*128+128]=(a+b).astype(BF)
+                L[cp,128+r:128+r+RC,q*128:q*128+128]=(a-b).astype(BF)
+
+def dots2i(tab,L): return [dot(L[cp],tab[3,cp]) for cp in range(2)]
+
+def space(D,r,n,q,uc):
+    a=D[0][r:r+n,q*128:q*128+128]; b=D[1][r:r+n,q*128:q*128+128]
+    return a+b if uc==0 else a-b
+
+def put2(P,q,r,sl,x0,x1):
+    P[0,q*128+r:q*128+r+RC,sl]=(x0+x1).astype(BF)
+    P[1,q*128+r:q*128+r+RC,sl]=(x0-x1).astype(BF)
+
+def putf(P,q,r,sl,x):
+    P[r//128,q*128+r%128:q*128+r%128+RC,sl]=x.astype(BF)
+
+def halves(r): return (slice(r,r+RC),slice(128+r,128+r+RC))
+def lanes(k): return slice(k*128,k*128+128)
+
+def phase_a(m,tab,pr,o0,kk,P,L,psi1):
+    for r in range(0,128,RC):
+        for uc in range(2):
+            sl=lanes(uc); xr=[];xi=[]
+            for h in halves(r):
+                a=pr[m,0,h,sl].astype(F32); b=pr[m,1,h,sl].astype(F32)
+                c=o0[0,h,sl].astype(F32); d=o0[1,h,sl].astype(F32)
+                xr.append(a*c-b*d); xi.append(a*d+b*c)
+            put2(P,0,r,sl,*xr); put2(P,1,r,sl,*xi)
+    V=dots1f(tab,P); yield
+    post1f(V,L); SS=dots2f(tab,L); yield
+    for r in range(0,256,RC):
         for cp in range(2):
-            a=E0[q*128:q*128+128,cp*128:cp*128+128]; b=E1[q*128:q*128+128,cp*128:cp*128+128]
-            L[cp,0:128,q*128:q*128+128]=(a+b).astype(BF)
-            L[cp,128:256,q*128:q*128+128]=(a-b).astype(BF)
-
-def s2f(tab,L,cp): return dot(L[cp],tab[2,cp])
-def s2i(tab,L):
-    D0=dot(L[0],tab[3,0]); D1=dot(L[1],tab[3,1])
-    return [[D0[:,q*128:q*128+128]+D1[:,q*128:q*128+128], D0[:,q*128:q*128+128]-D1[:,q*128:q*128+128]] for q in range(2)]
-
-def put_rows(P,q,uc,x):
-    a=x[:128]; b=x[128:]
-    P[0,q*128:q*128+128,uc*128:uc*128+128]=(a+b).astype(BF)
-    P[1,q*128:q*128+128,uc*128:uc*128+128]=(a-b).astype(BF)
-
-def put_freq(P,q,cp,x):
-    P[0,q*128:q*128+128,cp*128:cp*128+128]=x[:128].astype(BF)
-    P[1,q*128:q*128+128,cp*128:cp*128+128]=x[128:].astype(BF)
-
-def phase_a(m,tab,pr,o0,kk,P,L,psi1):
-    for uc in range(2):
-        sl=slice(uc*128,uc*128+128)
-        a=pr[m,0,:,sl].astype(F32); b=pr[m,1,:,sl].astype(F32)
-        c=o0[0,:,sl].astype(F32); d=o0[1,:,sl].astype(F32)
-        put_rows(P,0,uc,a*c-b*d); put_rows(P,1,uc,a*d+b*c)
-    s1f(tab,P,L)
-    for cp in range(2):
-        S=s2f(tab,L,cp)
-        sl=slice(cp*128,cp*128+128)
-        kr=kk[0,:,sl]; ki=kk[1,:,sl]
-        put_freq(P,0,cp,S[:,:128]*kr-S[:,128:]*ki)
-        put_freq(P,1,cp,S[:,:128]*ki+S[:,128:]*kr)
-    s1i(tab,P,L)
-    D=s2i(tab,L)
-    for uc in range(2):
-        sl=slice(uc*128,uc*128+128)
-        for q in range(2): psi1[m,q,:,sl]=D[q][uc]
+            S=SS[cp][r:r+RC]; sl=lanes(cp)
+            kr=kk[0,r:r+RC,sl]; ki=kk[1,r:r+RC,sl]
+            putf(P,0,r,sl,S[:,:128]*kr-S[:,128:]*ki)
+            putf(P,1,r,sl,S[:,:128]*ki+S[:,128:]*kr)
+    E=dots1i(tab,P); yield
+    post1i(E,L); D=dots2i(tab,L); yield
+    for r in range(0,256,RC):
+        for uc in range(2):
+            for q in range(2): psi1[m,q,r:r+RC,lanes(uc)]=space(D,r,RC,q,uc)
 
 def phase_b(m,tab,o1,P,L,psi1,far,inten):
-    for uc in range(2):
-        sl=slice(uc*128,uc*128+128)
-        a=psi1[m,0,:,sl]; b=psi1[m,1,:,sl]
-        c=o1[0,:,sl].astype(F32); d=o1[1,:,sl].astype(F32)
-        put_rows(P,0,uc,a*c-b*d); put_rows(P,1,uc,a*d+b*c)
-    s1f(tab,P,L)
-    for cp in range(2):
-        S=s2f(tab,L,cp)
-        far[m,cp]=S
-        inten[cp]+=S[:,:128]*S[:,:128]+S[:,128:]*S[:,128:]
+    for r in range(0,128,RC):
+        for uc in range(2):
+            sl=lanes(uc); xr=[];xi=[]
+            for h in halves(r):
+                a=psi1[m,0,h,sl]; b=psi1[m,1,h,sl]
+                c=o1[0,h,sl].astype(F32); d=o1[1,h,sl].astype(F32)
+                xr.append(a*c-b*d); xi.append(a*d+b*c)
+            put2(P,0,r,sl,*xr); put2(P,1,r,sl,*xi)
+    V=dots1f(tab,P); yield
+    post1f(V,L); SS=dots2f(tab,L); yield
+    for r in range(0,256,RC):
+        for cp in range(2):
+            S=SS[cp][r:r+RC]
+            far[m,cp,r:r+RC]=S
+            inten[cp,r:r+RC]+=S[:,:128]*S[:,:128]+S[:,128:]*S[:,128:]
 
 def phase_c(m,tab,o1,P,L,psi1,far,inten,g1,adj):
-    for cp in range(2):
-        w=inten[cp]
-        put_freq(P,0,cp,w*far[m,cp,:,:128]); put_freq(P,1,cp,w*far[m,cp,:,128:])
-    s1i(tab,P,L)
-    D=s2i(tab,L)
-    for uc in range(2):
-        sl=slice(uc*128,uc*128+128)
-        br=D[0][uc]; bi=D[1][uc]
-        a=psi1[m,0,:,sl]; b=psi1[m,1,:,sl]
-        g1[0,:,sl]+=a*br+b*bi; g1[1,:,sl]+=a*bi-b*br
-        c=o1[0,:,sl].astype(F32); d=o1[1,:,sl].astype(F32)
-        put_rows(adj.at[m],0,uc,c*br+d*bi); put_rows(adj.at[m],1,uc,c*bi-d*br)
+    for r in range(0,256,RC):
+        for cp in range(2):
+            w=inten[cp,r:r+RC]
+            putf(P,0,r,lanes(cp),w*far[m,cp,r:r+RC,:128]); putf(P,1,r,lanes(cp),w*far[m,cp,r:r+RC,128:])
+    E=dots1i(tab,P); yield
+    post1i(E,L); D=dots2i(tab,L); yield
+    for r in range(0,128,RC):
+        for uc in range(2):
+            sl=lanes(uc); ar=[];ai=[]
+            for h in halves(r):
+                br=space(D,h.start,RC,0,uc); bi=space(D,h.start,RC,1,uc)
+                a=psi1[m,0,h,sl]; b=psi1[m,1,h,sl]
+                g1[0,h,sl]+=a*br+b*bi; g1[1,h,sl]+=a*bi-b*br
+                c=o1[0,h,sl].astype(F32); d=o1[1,h,sl].astype(F32)
+                ar.append(c*br+d*bi); ai.append(c*bi-d*br)
+            put2(adj.at[m],0,r,sl,*ar); put2(adj.at[m],1,r,sl,*ai)
 
 def phase_d(m,tab,kk,P,L,L2,adj):
-    s1f(tab,adj.at[m],L)
-    for cp in range(2):
-        S=s2f(tab,L,cp).astype(BF).astype(F32)
-        sl=slice(cp*128,cp*128+128)
-        kr=kk[0,:,sl]; ki=kk[1,:,sl]
-        put_freq(P,0,cp,kr*S[:,:128]+ki*S[:,128:])
-        put_freq(P,1,cp,kr*S[:,128:]-ki*S[:,:128])
-    E0=dot(tab[1,0],P[0]); E1=dot(tab[1,1],P[1])
+    V=dots1f(tab,adj.at[m]); yield
+    post1f(V,L); SS=dots2f(tab,L); yield
+    for r in range(0,256,RC):
+        for cp in range(2):
+            S=SS[cp][r:r+RC].astype(BF).astype(F32); sl=lanes(cp)
+            kr=kk[0,r:r+RC,sl]; ki=kk[1,r:r+RC,sl]
+            putf(P,0,r,sl,kr*S[:,:128]+ki*S[:,128:])
+            putf(P,1,r,sl,kr*S[:,128:]-ki*S[:,:128])
+    E0,E1=dots1i(tab,P); yield
     for q in range(2):
-        for cp in range(2):
-            for h in range(2):
-                r=slice(q*128+h*64,q*128+h*64+64); sl=slice(cp*128,cp*128+128); to=slice(q*128,q*128+128)
-                L2[cp,h,m,:,to]=(E0[r,sl]+E1[r,sl]).astype(BF)
-                L2[cp,2+h,m,:,to]=(E0[r,sl]-E1[r,sl]).astype(BF)
+        for r in range(0,128,RC):
+            for cp in range(2):
+                rr=slice(q*128+r,q*128+r+RC); sl=lanes(cp); to=lanes(q); h=r//64; k=r%64
+                L2[cp,h,m,k:k+RC,to]=(E0[rr,sl]+E1[rr,sl]).astype(BF)
+                L2[cp,2+h,m,k:k+RC,to]=(E0[rr,sl]-E1[rr,sl]).astype(BF)
 
 def phase_e(r,tab,pr,L2,gs):
-    D0=dot(L2[0,r].reshape(256,256),tab[3,0]); D1=dot(L2[1,r].reshape(256,256),tab[3,1])
-    rows=slice(r*64,r*64+64)
-    for uc in range(2):
-        sl=slice(uc*128,uc*128+128)
-        W=[D0[:,q*128:q*128+128]+D1[:,q*128:q*128+128] if uc==0 else D0[:,q*128:q*128+128]-D1[:,q*128:q*128+128] for q in range(2)]
-        gr=None
-        for m in range(4):
-            wr=W[0][m*64:m*64+64]; wi=W[1][m*64:m*64+64]
-            a=pr[m,0,rows,sl].astype(F32); b=pr[m,1,rows,sl].astype(F32)
-            tr=a*wr+b*wi; ti=a*wi-b*wr
-            gr,gi=(tr,ti) if gr is None else (gr+tr,gi+ti)
-        gs[0,rows,sl]=gr.astype(BF); gs[1,rows,sl]=gi.astype(BF)
+    D=(dot(L2[0,r].reshape(256,256),tab[3,0]), dot(L2[1,r].reshape(256,256),tab[3,1])); yield
+    for k in range(0,64,RC):
+        rows=slice(r*64+k,r*64+k+RC)
+        for uc in range(2):
+            sl=lanes(uc)
+            gr=None
+            for m in range(4):
+                wr=space(D,m*64+k,RC,0,uc); wi=space(D,m*64+k,RC,1,uc)
+                a=pr[m,0,rows,sl].astype(F32); b=pr[m,1,rows,sl].astype(F32)
+                tr=a*wr+b*wi; ti=a*wi-b*wr
+                gr,gi=(tr,ti) if gr is None else (gr+tr,gi+ti)
+            gs[0,rows,sl]=gr.astype(BF); gs[1,rows,sl]=gi.astype(BF)
+
+
+def weave(items,width=2):
+    todo=list(items); live=[]
+    while todo or live:
+        if todo and len(live)<width:
+            item=todo.pop(0)
+            if item[0] is not None: item[0]()
+        else:
+            item=live.pop(0)
+        try:
+            next(item[1])
+            live.append(item)
+        except StopIteration:
+            if item[2] is not None: item[2]()
 
 
 MESH = pl.DeviceIdType.MESH
@@ -288,11 +326,13 @@
     def merge(s):
         for part in range(2):
             ob[s, part] = jnp.where(near_mask, near[s, part].astype(F32),
-                                    farw[s, part].astype(F32)).astype(BF)
-
-    def loop(f):
-        for m in range(MODES):
-            f(m)
+                                    farw[s, part].astype(F32))
+
+    def bufs(m):
+        return P.at[m % WIDTH], L.at[m % WIDTH]
+
+    def run(gens):
+        weave([(None, x, None) for x in gens], WIDTH)
 
     c_part.wait_recv()
 
@@ -303,10 +343,10 @@
 
     got_far(0)
     merge(0)
-    loop(lambda m: phase_a(m, tab, pr, ob.at[0], kk, P, L, psi1))
+    run([phase_a(m, tab, pr, ob.at[0], kk, *bufs(m), psi1) for m in range(MODES)])
     got_far(1)
     merge(1)
-    loop(lambda m: phase_b(m, tab, ob.at[1], P, L, psi1, far, inten))
+    run([phase_b(m, tab, ob.at[1], *bufs(m), psi1, far, inten) for m in range(MODES)])
 
     @pl.when(d == 1)
     def _():
@@ -315,7 +355,7 @@
     prep_meas(meas.at[d], mp)
     for cp in range(2):
         inten[cp] = (inten[cp] - mp[:, cp * 128:cp * 128 + 128]) * 0.125
-    loop(lambda m: phase_c(m, tab, ob.at[1], P, L, psi1, far, inten, g, adj))
+    run([phase_c(m, tab, ob.at[1], *bufs(m), psi1, far, inten, g, adj) for m in range(MODES)])
 
     gs[1] = g[...].astype(BF)
     far1 = remote(gs.at[1], out.at[2 + d], g_send.at[0], g_recv.at[2 + d], (1, nb))
@@ -334,7 +374,7 @@
     def _():
         stay1.start()
 
-    loop(lambda m: phase_d(m, tab, kk, P, L, L2, adj))
+    run([phase_d(m, tab, kk, *bufs(m), L2, adj) for m in range(MODES)])
 
     def chunk(r, dev):
         rows = pl.ds(r * 64, 64)
@@ -345,13 +385,12 @@
         return remote(gs.at[0, :, rows, :], out.at[2 + slot, :, rows, :], c_send.at[r], c_recv.at[slot, r],
                       (0, nb))
 
-    for r in range(4):
-        phase_e(r, tab, pr, L2, gs.at[0])
-
+    def ship(r):
         @pl.when(jnp.logical_not(wrap_a))
         def _():
             chunk(r, (0, nb)).start()
 
+    weave([(None, phase_e(r, tab, pr, L2, gs.at[0]), functools.partial(ship, r)) for r in range(4)], 2)
     near0 = remote(gs.at[0], out.at[d], g_send.at[1], g_recv.at[d], (0, p))
     stay0 = pltpu.make_async_copy(gs.at[0], out.at[d], loc_sem)
 
@@ -448,9 +487,9 @@
         out_specs=any_,
         scratch_shapes=[
             pltpu.SMEM((2, 2 * chips), jnp.int32), V((2, blocks, N, N), BF), win, win, win, V((2, 2, N, N), BF), V((2, 2, N, N), BF),
-            V((2, 2, N, N), BF), V((4, 2, N, N), BF), V((N, N), F32), V((2, N, N), BF), V((N, N), F32),
-            V((512, N), BF), V((N, 512), BF), V((4, 2, N, N), BF), V((4, 2, N, N), BF),
-            V((2, N, N), F32), V((N, N), F32), V((2, N, N), BF), V((2, N, N), BF),
+            V((2, 2, N, N), F32), V((4, 2, N, N), BF), V((N, N), F32), V((2, N, N), BF), V((N, N), F32),
+            V((512, N), BF), V((N, 512), BF), V((4, 2, N, N), BF), V((4, 2, N, N), F32),
+            V((2, N, N), F32), V((N, N), F32), V((WIDTH, 2, N, N), BF), V((WIDTH, 2, N, N), BF),
             V((4, 2, N, N), F32), V((4, 2, N, N), F32), V((2, N, 128), F32), V((4, 2, N, N), BF),
             V((2, 4, 4, 64, N), BF), V((2, N, N), F32), V((2, 2, N, N), BF),
             dma((7,)), dma((2,)), dma((2,)), dma, dma, dma, dma, dma((2,)), dma((4,)), dma((4,)), dma((2, 4)), dma, pltpu.SemaphoreType.REGULAR,

time: 37.1 us -> 36.1 us (0.973)
  Pallas kernels: 37 us -> 36 us
    pallas_call x1, Pallas kernels: 34.1 us -> 33.1 us  [local(): pl.pallas_call(functools.partial(main_kernel, chips, height), out_shape=j...]
where the time goes in v4:
time: 36.1 us; the launch traced here: 36 us
  Pallas kernels  36 us (100%)
    pallas_call x1, Pallas kernels, local(): pl.pallas_call(functools.partial(main_kernel, chips, height), out_shape=j...  33.1 us
    pallas_call x1, Pallas kernels, local(): pl.pallas_call(functools.partial(final_kernel, chips, blocks), out_shape=...  2.88 us

profile of v4, /device:TPU:6, one launch (start us, length us, event | category | flops | bytes accessed | tf_op | source)
XLA Modules:
  0.0 36.0 jit_solution(7055466813643035765)
XLA Ops:
  0.0 33.1 %ptycho.1.slots = bf16[4,2,256,256]{3,2,1,0:T(8,128)(2,1)S(1)} custom-call(s32[2,256]{1,0:T(2,128)} %bitcast.4, bf16[2,8,256,256]{3,2,1,0:T(8,128)(2,1)} %bitcast.3, bf16[4,2,256,256]{3,2,1,0:T(8,128)(2,1)} %probe_h.1, f32[256,256]{1,0:T(8,128)} %phase_h.1, f32[2,256,256]{2,1,0:T(8,128)} %meas_h.1, bf16[512,256]{1,0:T(8,128)(2,1)} %constant.4.clone.tb_h, ...), custom_call_target="tpu_custom_call" | custom-call | tf_op jit(solution)/shard_map/ptycho/pallas_call | solution.py:483
  33.1 2.9 %assemble.1 = bf16[2,8,256,256]{3,2,1,0:T(8,128)(2,1)} custom-call(s32[2,256]{1,0:T(2,128)} %bitcast.5, bf16[4,2,256,256]{3,2,1,0:T(8,128)(2,1)S(1)} %ptycho.1.slots), custom_call_target="tpu_custom_call" | custom-call | tf_op jit(solution)/shard_map/assemble/pallas_call | solution.py:502

commit v5 on v4

--- a/solution.py
+++ b/solution.py
@@ -214,7 +214,7 @@
                 pos, band, w_left, w_right, w_part, near, farw, ob, probe, phase, meas, mtmp,
                 tb, tbt, tab, pr, kk, mp, P, L, psi1, far, inten, adj, L2, g, gs,
                 in_sem, obj_send, obj_recv, near_send, near_recv, m_send, m_recv,
-                g_send, g_recv, c_send, c_recv, loc_sem, turn):
+                g_send, g_recv, c_send, c_recv, loc_sem):
     d = lax.axis_index("depth")
     p = lax.axis_index("pos")
     left = lax.rem(p + chips - 1, chips)
@@ -265,56 +265,50 @@
         near[d, part] = window(mine, part)
     y = pos[0, mine] & 255
     c = pos[1, mine] & 255
+    pl.semaphore_wait(barrier, 4)
+
+    def remote(src, dst, ss, rs, dev):
+        return pltpu.make_async_remote_copy(src_ref=src, dst_ref=dst, send_sem=ss, recv_sem=rs,
+                                            device_id=dev, device_id_type=MESH)
+
+    c_left = remote(w_left, farw.at[d], obj_send.at[0], obj_recv.at[d], (0, left))
+    c_right = remote(w_right, farw.at[d], obj_send.at[1], obj_recv.at[d], (1, right))
+    c_part = remote(w_part, near.at[d], near_send, near_recv, (1 - d, p))
+    go_left = p > 0
+    wrap_a = jnp.logical_and(d == 0, p == chips - 1)
+
+    def send_object():
+        @pl.when(go_left)
+        def _():
+            c_left.start()
+
+        c_right.start()
+
+    def sent_object():
+        @pl.when(go_left)
+        def _():
+            c_left.wait_send()
+
+        c_right.wait_send()
+
+    @pl.when(d == 0)
+    def _():
+        send_object()
+
+    c_part.start()
+    loads[1].wait()
+    c_meas = remote(meas.at[0], meas.at[1], m_send, m_recv, (1, right))
+    meas[0] = mtmp[...].astype(BF)
     loads[2].wait()
     loads[3].wait()
     prep_tables(tb, tbt, tab, y, c)
     loads[4].wait()
     prep_probe(probe, pr, None, y, c)
-    pl.semaphore_wait(barrier, 4)
-
-    def remote(src, dst, ss, rs, dev):
-        return pltpu.make_async_remote_copy(src_ref=src, dst_ref=dst, send_sem=ss, recv_sem=rs,
-                                            device_id=dev, device_id_type=MESH)
-
-    c_left = remote(w_left, farw.at[d], obj_send.at[0], obj_recv.at[d], (0, left))
-    c_right = remote(w_right, farw.at[d], obj_send.at[1], obj_recv.at[d], (1, right))
-    c_part = remote(w_part, near.at[d], near_send, near_recv, (1 - d, p))
-    go_left = p > 0
-    wrap_a = jnp.logical_and(d == 0, p == chips - 1)
-
-    def send_object():
-        @pl.when(go_left)
-        def _():
-            c_left.start()
-
-        c_right.start()
-
-    def sent_object():
-        @pl.when(go_left)
-        def _():
-            c_left.wait_send()
-
-        c_right.wait_send()
-
-    @pl.when(d == 0)
-    def _():
-        send_object()
-
-    c_part.start()
-    loads[1].wait()
-    c_meas = remote(meas.at[0], meas.at[1], m_send, m_recv, (1, right))
-    meas[0] = mtmp[...].astype(BF)
     loads[5].wait()
     prep_k(phase, kk)
 
-    @pl.when(d == 0)
-    def _():
-        sent_object()
-        pl.semaphore_signal(turn, inc=1, device_id=(1, p), device_id_type=MESH)
-
     @pl.when(d == 1)
     def _():
-        pl.semaphore_wait(turn, 1)
         send_object()
         c_meas.start()
 
@@ -404,10 +398,7 @@
         stay0.start()
         near1.wait_send()
 
-    @pl.when(d == 1)
-    def _():
-        sent_object()
-
+    sent_object()
     c_part.wait_send()
 
     @pl.when(jnp.logical_not(wrap_a))
@@ -439,15 +430,15 @@
                 incoming(0, r).wait_recv()
 
 
-def final_kernel(chips, blocks, pos_h, slots, out, pos, acc, ob, sem, pos_sem):
+def final_kernel(chips, blocks, pos_h, slots, out, pos, acc, sem, pos_sem):
     load = pltpu.make_async_copy(pos_h, pos, pos_sem)
     load.start()
     p = lax.axis_index("pos")
     total = 2 * chips
     acc[...] = jnp.zeros_like(acc)
     load.wait()
-    rows = iota((N, N), 0)
-    cols = iota((N, N), 1)
+    rows = iota((16, N), 0)
+    cols = iota((16, N), 1)
     for slot, (off, ge) in enumerate(((0, True), (total - 1, False), (total - 2, False), (1, True))):
         q = lax.rem(2 * p + off, total)
         y = pos[0, q]
@@ -456,14 +447,21 @@
         yy = y & 255
         c = pos[1, q] & 255
         cm = (cols >= c) if ge else (cols < c)
+        for r0 in range(0, N, 16):
+            later = r0 + 15 < yy
+            to = jnp.where(later, k2, k)
+            keep = cm & (rows >= jnp.where(later, 0, yy - r0))
+            for part in range(2):
+                x = slots[slot, part, r0:r0 + 16]
+                acc[part, to, r0:r0 + 16] += jnp.where(keep, x, jnp.zeros_like(x))
+        rb = pl.multiple_of((yy >> 4) * 16, 16)
+        keep = cm & (rows < yy - rb)
         for part in range(2):
-            x = slots[slot, part].astype(F32)
-            acc[part, k] += jnp.where(cm & (rows >= yy), x, 0.0)
-            acc[part, k2] += jnp.where(cm & (rows < yy), x, 0.0)
+            x = slots[slot, part, pl.ds(rb, 16)]
+            acc[part, k2, pl.ds(rb, 16)] += jnp.where(keep, x, jnp.zeros_like(x))
     copies = []
     for i in range(blocks):
-        ob[:, i] = acc[:, i].astype(BF)
-        cp = pltpu.make_async_copy(ob.at[:, i], out.at[:, i], sem.at[i])
+        cp = pltpu.make_async_copy(acc.at[:, i], out.at[:, i], sem.at[i])
         cp.start()
         copies.append(cp)
     for cp in copies:
@@ -492,7 +490,7 @@
             V((2, N, N), F32), V((N, N), F32), V((WIDTH, 2, N, N), BF), V((WIDTH, 2, N, N), BF),
             V((4, 2, N, N), F32), V((4, 2, N, N), F32), V((2, N, 128), F32), V((4, 2, N, N), BF),
             V((2, 4, 4, 64, N), BF), V((2, N, N), F32), V((2, 2, N, N), BF),
-            dma((7,)), dma((2,)), dma((2,)), dma, dma, dma, dma, dma((2,)), dma((4,)), dma((4,)), dma((2, 4)), dma, pltpu.SemaphoreType.REGULAR,
+            dma((7,)), dma((2,)), dma((2,)), dma, dma, dma, dma, dma((2,)), dma((4,)), dma((4,)), dma((2, 4)), dma,
         ],
         compiler_params=pltpu.CompilerParams(
             collective_id=0, has_side_effects=True, vmem_limit_bytes=48 * 1024 * 1024),
@@ -504,8 +502,7 @@
         out_shape=jax.ShapeDtypeStruct((2, blocks, N, N), BF),
         in_specs=[pl.BlockSpec(memory_space=pltpu.HBM), pl.BlockSpec(memory_space=pltpu.VMEM)],
         out_specs=pl.BlockSpec(memory_space=pltpu.HBM),
-        scratch_shapes=[pltpu.SMEM((2, 2 * chips), jnp.int32), V((2, blocks, N, N), F32), V((2, blocks, N, N), BF),
-                        dma((blocks,)), dma],
+        scratch_shapes=[pltpu.SMEM((2, 2 * chips), jnp.int32), V((2, blocks, N, N), BF), dma((blocks,)), dma],
         compiler_params=pltpu.CompilerParams(vmem_limit_bytes=32 * 1024 * 1024),
         name="assemble",
     )(pltpu.with_memory_space_constraint(pos_t, pltpu.HBM), slots)

time: 36.1 us -> 34.8 us (0.964)
  Pallas kernels: 36 us -> 34.7 us
    pallas_call x1, Pallas kernels: 33.1 us -> 32.2 us  [local(): pl.pallas_call(functools.partial(main_kernel, chips, height), out_shape=j...]
    pallas_call x1, Pallas kernels: 2.88 us -> 2.46 us  [local(): pl.pallas_call(functools.partial(final_kernel, chips, blocks), out_shape=...]
where the time goes in v5:
time: 34.8 us; the launch traced here: 34.7 us
  Pallas kernels  34.7 us (100%)
    pallas_call x1, Pallas kernels, local(): pl.pallas_call(functools.partial(main_kernel, chips, height), out_shape=j...  32.2 us
    pallas_call x1, Pallas kernels, local(): pl.pallas_call(functools.partial(final_kernel, chips, blocks), out_shape=...  2.46 us

profile of v5, /device:TPU:6, one launch (start us, length us, event | category | flops | bytes accessed | tf_op | source)
XLA Modules:
  0.0 34.7 jit_solution(13020779737292002276)
XLA Ops:
  0.0 32.2 %ptycho.1.slots = bf16[4,2,256,256]{3,2,1,0:T(8,128)(2,1)S(1)} custom-call(s32[2,256]{1,0:T(2,128)} %bitcast.4, bf16[2,8,256,256]{3,2,1,0:T(8,128)(2,1)} %bitcast.3, bf16[4,2,256,256]{3,2,1,0:T(8,128)(2,1)} %probe_h.1, f32[256,256]{1,0:T(8,128)} %phase_h.1, f32[2,256,256]{2,1,0:T(8,128)} %meas_h.1, bf16[512,256]{1,0:T(8,128)(2,1)} %constant.4.clone.tb_h, ...), custom_call_target="tpu_custom_call" | custom-call | tf_op jit(solution)/shard_map/ptycho/pallas_call | solution.py:481
  32.2 2.5 %assemble.1 = bf16[2,8,256,256]{3,2,1,0:T(8,128)(2,1)} custom-call(s32[2,256]{1,0:T(2,128)} %bitcast.5, bf16[4,2,256,256]{3,2,1,0:T(8,128)(2,1)S(1)} %ptycho.1.slots), custom_call_target="tpu_custom_call" | custom-call | tf_op jit(solution)/shard_map/assemble/pallas_call | solution.py:500

commit v6 on v5

--- a/solution.py
+++ b/solution.py
@@ -142,23 +142,36 @@
             far[m,cp,r:r+RC]=S
             inten[cp,r:r+RC]+=S[:,:128]*S[:,:128]+S[:,128:]*S[:,128:]
 
-def phase_c(m,tab,o1,P,L,psi1,far,inten,g1,adj):
+def phase_c(m,tab,P,L3,far,inten):
     for r in range(0,256,RC):
         for cp in range(2):
             w=inten[cp,r:r+RC]
             putf(P,0,r,lanes(cp),w*far[m,cp,r:r+RC,:128]); putf(P,1,r,lanes(cp),w*far[m,cp,r:r+RC,128:])
-    E=dots1i(tab,P); yield
-    post1i(E,L); D=dots2i(tab,L); yield
-    for r in range(0,128,RC):
-        for uc in range(2):
-            sl=lanes(uc); ar=[];ai=[]
-            for h in halves(r):
-                br=space(D,h.start,RC,0,uc); bi=space(D,h.start,RC,1,uc)
+    E0,E1=dots1i(tab,P); yield
+    for q in range(2):
+        for r in range(4):
+            for cp in range(2):
+                rr=slice(q*128+r*32,q*128+r*32+32); sl=lanes(cp); to=lanes(q)
+                L3[cp,r,m,0:32,to]=(E0[rr,sl]+E1[rr,sl]).astype(BF)
+                L3[cp,r,m,32:64,to]=(E0[rr,sl]-E1[rr,sl]).astype(BF)
+
+def phase_c2(r,tab,o1,L3,psi1,gs,adj):
+    D=[dot(L3[cp,r].reshape(256,256),tab[3,cp]) for cp in range(2)]; yield
+    for uc in range(2):
+        sl=lanes(uc); gr=[None,None]; gi=[None,None]
+        hs=(slice(r*32,r*32+32),slice(128+r*32,160+r*32))
+        for m in range(4):
+            ar=[];ai=[]
+            for k,h in enumerate(hs):
+                br=space(D,m*64+32*k,32,0,uc); bi=space(D,m*64+32*k,32,1,uc)
                 a=psi1[m,0,h,sl]; b=psi1[m,1,h,sl]
-                g1[0,h,sl]+=a*br+b*bi; g1[1,h,sl]+=a*bi-b*br
-                c=o1[0,h,sl].astype(F32); d=o1[1,h,sl].astype(F32)
+                tr=a*br+b*bi; ti=a*bi-b*br
+                gr[k]=tr if m==0 else gr[k]+tr; gi[k]=ti if m==0 else gi[k]+ti
+                c=o1[0,h,sl]; d=o1[1,h,sl]
                 ar.append(c*br+d*bi); ai.append(c*bi-d*br)
-            put2(adj.at[m],0,r,sl,*ar); put2(adj.at[m],1,r,sl,*ai)
+            put2(adj.at[m],0,r*32,sl,*ar); put2(adj.at[m],1,r*32,sl,*ai)
+        for k,h in enumerate(hs):
+            gs[0,h,sl]=gr[k].astype(BF); gs[1,h,sl]=gi[k].astype(BF)
 
 def phase_d(m,tab,kk,P,L,L2,adj):
     V=dots1f(tab,adj.at[m]); yield
@@ -212,9 +225,9 @@
 
 def main_kernel(chips, height, pos_h, obj, probe_h, phase_h, meas_h, tb_h, tbt_h, out,
                 pos, band, w_left, w_right, w_part, near, farw, ob, probe, phase, meas, mtmp,
-                tb, tbt, tab, pr, kk, mp, P, L, psi1, far, inten, adj, L2, g, gs,
+                tb, tbt, tab, pr, kk, mp, P, L, psi1, far, inten, adj, L2, L3, gs,
                 in_sem, obj_send, obj_recv, near_send, near_recv, m_send, m_recv,
-                g_send, g_recv, c_send, c_recv, loc_sem):
+                g_send, g_recv, h_send, h_recv, c_send, c_recv, loc_sem):
     d = lax.axis_index("depth")
     p = lax.axis_index("pos")
     left = lax.rem(p + chips - 1, chips)
@@ -313,7 +326,6 @@
         c_meas.start()
 
     inten[...] = jnp.zeros_like(inten)
-    g[...] = jnp.zeros_like(g)
 
     near_mask = (iota((N, N), 1) - c) * (1 - 2 * d) - d >= 0
 
@@ -349,16 +361,23 @@
     prep_meas(meas.at[d], mp)
     for cp in range(2):
         inten[cp] = (inten[cp] - mp[:, cp * 128:cp * 128 + 128]) * 0.125
-    run([phase_c(m, tab, ob.at[1], *bufs(m), psi1, far, inten, g, adj) for m in range(MODES)])
-
-    gs[1] = g[...].astype(BF)
-    far1 = remote(gs.at[1], out.at[2 + d], g_send.at[0], g_recv.at[2 + d], (1, nb))
+    run([phase_c(m, tab, P.at[m], L3, far, inten) for m in range(MODES)])
+
+    def strip(slot, i, dev):
+        rows = pl.ds(i * 32, 32)
+        return remote(gs.at[1, :, rows, :], out.at[2 + slot, :, rows, :], h_send.at[i], h_recv.at[slot, i], dev)
+
+    def ship1(r):
+        @pl.when(jnp.logical_not(wrap_a))
+        def _():
+            strip(d, r, (1, nb)).start()
+            strip(d, r + 4, (1, nb)).start()
+
+    weave([(None, phase_c2(r, tab, ob.at[1], L3, psi1, gs.at[1], adj), functools.partial(ship1, r))
+           for r in range(4)], 2)
+
     near1 = remote(gs.at[1], out.at[d], g_send.at[1], g_recv.at[d], (1, p))
     stay1 = pltpu.make_async_copy(gs.at[1], out.at[d], loc_sem)
-
-    @pl.when(jnp.logical_not(wrap_a))
-    def _():
-        far1.start()
 
     @pl.when(d == 0)
     def _():
@@ -403,7 +422,8 @@
 
     @pl.when(jnp.logical_not(wrap_a))
     def _():
-        far1.wait_send()
+        for i in range(8):
+            strip(d, i, (1, nb)).wait_send()
         for r in range(4):
             chunk(r, (0, nb)).wait_send()
 
@@ -411,11 +431,13 @@
     def _():
         near0.wait_send()
         remote(gs.at[1], out.at[0], g_send.at[1], g_recv.at[0], (0, p)).wait_recv()
-        remote(gs.at[1], out.at[3], g_send.at[0], g_recv.at[3], (1, nb)).wait_recv()
+        for i in range(8):
+            strip(1, i, (1, nb)).wait_recv()
 
         @pl.when(p > 0)
         def _():
-            remote(gs.at[1], out.at[2], g_send.at[0], g_recv.at[2], (1, nb)).wait_recv()
+            for i in range(8):
+                strip(0, i, (1, nb)).wait_recv()
 
     @pl.when(d == 0)
     def _():
@@ -439,29 +461,27 @@
     load.wait()
     rows = iota((16, N), 0)
     cols = iota((16, N), 1)
-    for slot, (off, ge) in enumerate(((0, True), (total - 1, False), (total - 2, False), (1, True))):
+    places = []
+    for off, ge in ((0, True), (total - 1, False), (total - 2, False), (1, True)):
         q = lax.rem(2 * p + off, total)
         y = pos[0, q]
+        c = pos[1, q] & 255
         k = y >> 8
-        k2 = jnp.minimum(k + 1, blocks - 1)
-        yy = y & 255
-        c = pos[1, q] & 255
-        cm = (cols >= c) if ge else (cols < c)
-        for r0 in range(0, N, 16):
-            later = r0 + 15 < yy
-            to = jnp.where(later, k2, k)
-            keep = cm & (rows >= jnp.where(later, 0, yy - r0))
-            for part in range(2):
+        places.append((k, jnp.minimum(k + 1, blocks - 1), y & 255, (cols >= c) if ge else (cols < c)))
+    copies = []
+    for part in range(2):
+        for slot, (k, k2, yy, cm) in enumerate(places):
+            for r0 in range(0, N, 16):
+                later = r0 + 15 < yy
+                to = jnp.where(later, k2, k)
+                keep = cm & (rows >= jnp.where(later, 0, yy - r0))
                 x = slots[slot, part, r0:r0 + 16]
                 acc[part, to, r0:r0 + 16] += jnp.where(keep, x, jnp.zeros_like(x))
-        rb = pl.multiple_of((yy >> 4) * 16, 16)
-        keep = cm & (rows < yy - rb)
-        for part in range(2):
+            rb = pl.multiple_of((yy >> 4) * 16, 16)
+            keep = cm & (rows < yy - rb)
             x = slots[slot, part, pl.ds(rb, 16)]
             acc[part, k2, pl.ds(rb, 16)] += jnp.where(keep, x, jnp.zeros_like(x))
-    copies = []
-    for i in range(blocks):
-        cp = pltpu.make_async_copy(acc.at[:, i], out.at[:, i], sem.at[i])
+        cp = pltpu.make_async_copy(acc.at[part], out.at[part], sem.at[part])
         cp.start()
         copies.append(cp)
     for cp in copies:
@@ -489,8 +509,9 @@
             V((512, N), BF), V((N, 512), BF), V((4, 2, N, N), BF), V((4, 2, N, N), F32),
             V((2, N, N), F32), V((N, N), F32), V((WIDTH, 2, N, N), BF), V((WIDTH, 2, N, N), BF),
             V((4, 2, N, N), F32), V((4, 2, N, N), F32), V((2, N, 128), F32), V((4, 2, N, N), BF),
-            V((2, 4, 4, 64, N), BF), V((2, N, N), F32), V((2, 2, N, N), BF),
-            dma((7,)), dma((2,)), dma((2,)), dma, dma, dma, dma, dma((2,)), dma((4,)), dma((4,)), dma((2, 4)), dma,
+            V((2, 4, 4, 64, N), BF), V((2, 4, 4, 64, N), BF), V((2, 2, N, N), BF),
+            dma((7,)), dma((2,)), dma((2,)), dma, dma, dma, dma,
+            dma((2,)), dma((4,)), dma((8,)), dma((2, 8)), dma((4,)), dma((2, 4)), dma,
         ],
         compiler_params=pltpu.CompilerParams(
             collective_id=0, has_side_effects=True, vmem_limit_bytes=48 * 1024 * 1024),
@@ -500,12 +521,12 @@
     band = pl.pallas_call(
         functools.partial(final_kernel, chips, blocks),
         out_shape=jax.ShapeDtypeStruct((2, blocks, N, N), BF),
-        in_specs=[pl.BlockSpec(memory_space=pltpu.HBM), pl.BlockSpec(memory_space=pltpu.VMEM)],
+        in_specs=[any_, pl.BlockSpec(memory_space=pltpu.VMEM)],
         out_specs=pl.BlockSpec(memory_space=pltpu.HBM),
-        scratch_shapes=[pltpu.SMEM((2, 2 * chips), jnp.int32), V((2, blocks, N, N), BF), dma((blocks,)), dma],
+        scratch_shapes=[pltpu.SMEM((2, 2 * chips), jnp.int32), V((2, blocks, N, N), BF), dma((2,)), dma],
         compiler_params=pltpu.CompilerParams(vmem_limit_bytes=32 * 1024 * 1024),
         name="assemble",
-    )(pltpu.with_memory_space_constraint(pos_t, pltpu.HBM), slots)
+    )(pos_t, slots)
     return band.reshape(1, 2, height, N)
 
 

time: 34.8 us -> 34.3 us (0.986)
  Pallas kernels: 34.7 us -> 34.2 us
where the time goes in v6:
time: 34.3 us; the launch traced here: 34.2 us
  Pallas kernels  34.2 us (100%)
    pallas_call x1, Pallas kernels, local(): pl.pallas_call(functools.partial(main_kernel, chips, height), out_shape=j...  31.9 us
    pallas_call x1, Pallas kernels, local(): pl.pallas_call(functools.partial(final_kernel, chips, blocks), out_shape=...  2.27 us

profile of v6, /device:TPU:6, one launch (start us, length us, event | category | flops | bytes accessed | tf_op | source)
XLA Modules:
  0.0 34.2 jit_solution(9231833519096650967)
XLA Ops:
  0.0 0.0 copy-start
  0.0 31.9 %ptycho.1.slots = bf16[4,2,256,256]{3,2,1,0:T(8,128)(2,1)S(1)} custom-call(s32[2,256]{1,0:T(2,128)} %bitcast.3, bf16[2,8,256,256]{3,2,1,0:T(8,128)(2,1)} %bitcast.5, bf16[4,2,256,256]{3,2,1,0:T(8,128)(2,1)} %probe_h.1, f32[256,256]{1,0:T(8,128)} %phase_h.1, f32[2,256,256]{2,1,0:T(8,128)} %meas_h.1, bf16[512,256]{1,0:T(8,128)(2,1)} %constant.4.clone.tb_h, ...), custom_call_target="tpu_custom_call" | custom-call | tf_op jit(solution)/shard_map/ptycho/pallas_call | solution.py:501
  31.9 0.0 copy-done
  31.9 2.3 %assemble.1 = bf16[2,8,256,256]{3,2,1,0:T(8,128)(2,1)} custom-call(s32[2,256]{1,0:T(2,128)S(1)} %bitcast.4, bf16[4,2,256,256]{3,2,1,0:T(8,128)(2,1)S(1)} %ptycho.1.slots), custom_call_target="tpu_custom_call" | custom-call | tf_op jit(solution)/shard_map/assemble/pallas_call | solution.py:521
Async XLA Ops:
  0.0 31.9 %copy-start = (s32[256,2]{0,1:T(2,128)S(1)}, s32[256,2]{0,1:T(2,128)}, u32[]{:S(2)}) copy-start(s32[256,2]{0,1:T(2,128)} %param.11) | copy-start | bytes 6148

commit v7 on v6

--- a/solution.py
+++ b/solution.py
@@ -239,6 +239,11 @@
     q_left = lax.rem(2 * p - 2 + total, total)
     q_right = 2 * p + 1
 
+    barrier = pltpu.get_barrier_semaphore()
+    peers = ((1 - d, p), (0, left), (1, right), (d, nb))
+    for peer in peers:
+        pl.semaphore_signal(barrier, inc=1, device_id=peer, device_id_type=MESH)
+
     loads = [
         pltpu.make_async_copy(obj, band, in_sem.at[0]),
         pltpu.make_async_copy(meas_h.at[d], mtmp, in_sem.at[1]),
@@ -250,10 +255,6 @@
     ]
     for cp in loads:
         cp.start()
-    barrier = pltpu.get_barrier_semaphore()
-    peers = ((1 - d, p), (0, left), (1, right), (d, nb))
-    for peer in peers:
-        pl.semaphore_signal(barrier, inc=1, device_id=peer, device_id_type=MESH)
 
     blocks = height // N
     row_id = iota((N, N), 0)
@@ -274,8 +275,6 @@
         w_right[part] = window(q_right, part)
     for part in range(2):
         w_part[part] = window(other, part)
-    for part in range(2):
-        near[d, part] = window(mine, part)
     y = pos[0, mine] & 255
     c = pos[1, mine] & 255
     pl.semaphore_wait(barrier, 4)
@@ -319,13 +318,15 @@
     prep_probe(probe, pr, None, y, c)
     loads[5].wait()
     prep_k(phase, kk)
+    for part in range(2):
+        near[d, part] = window(mine, part)
+    inten[...] = jnp.zeros_like(inten)
 
     @pl.when(d == 1)
     def _():
         send_object()
         c_meas.start()
 
-    inten[...] = jnp.zeros_like(inten)
 
     near_mask = (iota((N, N), 1) - c) * (1 - 2 * d) - d >= 0
 
@@ -471,17 +472,17 @@
     copies = []
     for part in range(2):
         for slot, (k, k2, yy, cm) in enumerate(places):
-            for r0 in range(0, N, 16):
-                later = r0 + 15 < yy
-                to = jnp.where(later, k2, k)
-                keep = cm & (rows >= jnp.where(later, 0, yy - r0))
-                x = slots[slot, part, r0:r0 + 16]
-                acc[part, to, r0:r0 + 16] += jnp.where(keep, x, jnp.zeros_like(x))
+            to = [jnp.where(r0 + 15 < yy, k2, jnp.where(r0 >= yy, k, blocks)) for r0 in range(0, N, 16)]
+            old = [acc[part, to[i], 16 * i:16 * i + 16] for i in range(N // 16)]
+            for i in range(N // 16):
+                x = slots[slot, part, 16 * i:16 * i + 16]
+                acc[part, to[i], 16 * i:16 * i + 16] = old[i] + jnp.where(cm, x, jnp.zeros_like(x))
             rb = pl.multiple_of((yy >> 4) * 16, 16)
-            keep = cm & (rows < yy - rb)
             x = slots[slot, part, pl.ds(rb, 16)]
-            acc[part, k2, pl.ds(rb, 16)] += jnp.where(keep, x, jnp.zeros_like(x))
-        cp = pltpu.make_async_copy(acc.at[part], out.at[part], sem.at[part])
+            here = rows >= jnp.where((yy & 15) != 0, yy - rb, N)
+            acc[part, k, pl.ds(rb, 16)] += jnp.where(cm & here, x, jnp.zeros_like(x))
+            acc[part, k2, pl.ds(rb, 16)] += jnp.where(cm & (rows < yy - rb), x, jnp.zeros_like(x))
+        cp = pltpu.make_async_copy(acc.at[part, 0:blocks], out.at[part], sem.at[part])
         cp.start()
         copies.append(cp)
     for cp in copies:
@@ -523,7 +524,7 @@
         out_shape=jax.ShapeDtypeStruct((2, blocks, N, N), BF),
         in_specs=[any_, pl.BlockSpec(memory_space=pltpu.VMEM)],
         out_specs=pl.BlockSpec(memory_space=pltpu.HBM),
-        scratch_shapes=[pltpu.SMEM((2, 2 * chips), jnp.int32), V((2, blocks, N, N), BF), dma((2,)), dma],
+        scratch_shapes=[pltpu.SMEM((2, 2 * chips), jnp.int32), V((2, blocks + 1, N, N), BF), dma((2,)), dma],
         compiler_params=pltpu.CompilerParams(vmem_limit_bytes=32 * 1024 * 1024),
         name="assemble",
     )(pos_t, slots)

time: 34.3 us -> 34.1 us (level)
  no operation moved by 1% of the time
where the time goes in v7:
time: 34.1 us; the launch traced here: 34 us
  Pallas kernels  34 us (100%)
    pallas_call x1, Pallas kernels, local(): pl.pallas_call(functools.partial(main_kernel, chips, height), out_shape=j...  31.9 us
    pallas_call x1, Pallas kernels, local(): pl.pallas_call(functools.partial(final_kernel, chips, blocks), out_shape=...  2.12 us

profile of v7, /device:TPU:6, one launch (start us, length us, event | category | flops | bytes accessed | tf_op | source)
XLA Modules:
  0.0 34.0 jit_solution(14926725319082054584)
XLA Ops:
  0.0 0.0 copy-start
  0.0 31.9 %ptycho.1.slots = bf16[4,2,256,256]{3,2,1,0:T(8,128)(2,1)S(1)} custom-call(s32[2,256]{1,0:T(2,128)} %bitcast.3, bf16[2,8,256,256]{3,2,1,0:T(8,128)(2,1)} %bitcast.5, bf16[4,2,256,256]{3,2,1,0:T(8,128)(2,1)} %probe_h.1, f32[256,256]{1,0:T(8,128)} %phase_h.1, f32[2,256,256]{2,1,0:T(8,128)} %meas_h.1, bf16[512,256]{1,0:T(8,128)(2,1)} %constant.4.clone.tb_h, ...), custom_call_target="tpu_custom_call" | custom-call | tf_op jit(solution)/shard_map/ptycho/pallas_call | solution.py:502
  31.9 0.0 copy-done
  31.9 2.1 %assemble.1 = bf16[2,8,256,256]{3,2,1,0:T(8,128)(2,1)} custom-call(s32[2,256]{1,0:T(2,128)S(1)} %bitcast.4, bf16[4,2,256,256]{3,2,1,0:T(8,128)(2,1)S(1)} %ptycho.1.slots), custom_call_target="tpu_custom_call" | custom-call | tf_op jit(solution)/shard_map/assemble/pallas_call | solution.py:522
Async XLA Ops:
  0.0 31.9 %copy-start = (s32[256,2]{0,1:T(2,128)S(1)}, s32[256,2]{0,1:T(2,128)}, u32[]{:S(2)}) copy-start(s32[256,2]{0,1:T(2,128)} %param.11) | copy-start | bytes 6148

commit v8 on v7

--- a/solution.py
+++ b/solution.py
@@ -341,6 +341,10 @@
     def run(gens):
         weave([(None, x, None) for x in gens], WIDTH)
 
+    @pl.when(d == 0)
+    def _():
+        prep_meas(meas.at[0], mp)
+
     c_part.wait_recv()
 
     def got_far(k):
@@ -358,8 +362,8 @@
     @pl.when(d == 1)
     def _():
         c_meas.wait()
-
-    prep_meas(meas.at[d], mp)
+        prep_meas(meas.at[1], mp)
+
     for cp in range(2):
         inten[cp] = (inten[cp] - mp[:, cp * 128:cp * 128 + 128]) * 0.125
     run([phase_c(m, tab, P.at[m], L3, far, inten) for m in range(MODES)])
@@ -482,9 +486,10 @@
             here = rows >= jnp.where((yy & 15) != 0, yy - rb, N)
             acc[part, k, pl.ds(rb, 16)] += jnp.where(cm & here, x, jnp.zeros_like(x))
             acc[part, k2, pl.ds(rb, 16)] += jnp.where(cm & (rows < yy - rb), x, jnp.zeros_like(x))
-        cp = pltpu.make_async_copy(acc.at[part, 0:blocks], out.at[part], sem.at[part])
-        cp.start()
-        copies.append(cp)
+        for i in range(0, blocks, 2):
+            cp = pltpu.make_async_copy(acc.at[part, i:i + 2], out.at[part, i:i + 2], sem.at[part, i // 2])
+            cp.start()
+            copies.append(cp)
     for cp in copies:
         cp.wait()
 
@@ -524,7 +529,7 @@
         out_shape=jax.ShapeDtypeStruct((2, blocks, N, N), BF),
         in_specs=[any_, pl.BlockSpec(memory_space=pltpu.VMEM)],
         out_specs=pl.BlockSpec(memory_space=pltpu.HBM),
-        scratch_shapes=[pltpu.SMEM((2, 2 * chips), jnp.int32), V((2, blocks + 1, N, N), BF), dma((2,)), dma],
+        scratch_shapes=[pltpu.SMEM((2, 2 * chips), jnp.int32), V((2, blocks + 1, N, N), BF), dma((2, blocks // 2)), dma],
         compiler_params=pltpu.CompilerParams(vmem_limit_bytes=32 * 1024 * 1024),
         name="assemble",
     )(pos_t, slots)

time: 34.1 us -> 34 us (level)
  no operation moved by 1% of the time
where the time goes in v8:
time: 34 us; the launch traced here: 33.9 us
  Pallas kernels  33.9 us (100%)
    pallas_call x1, Pallas kernels, local(): pl.pallas_call(functools.partial(main_kernel, chips, height), out_shape=j...  31.7 us
    pallas_call x1, Pallas kernels, local(): pl.pallas_call(functools.partial(final_kernel, chips, blocks), out_shape=...  2.16 us

profile of v8, /device:TPU:6, one launch (start us, length us, event | category | flops | bytes accessed | tf_op | source)
XLA Modules:
  0.0 33.9 jit_solution(13829890834916207160)
XLA Ops:
  0.0 0.0 copy-start
  0.0 31.7 %ptycho.1.slots = bf16[4,2,256,256]{3,2,1,0:T(8,128)(2,1)S(1)} custom-call(s32[2,256]{1,0:T(2,128)} %bitcast.3, bf16[2,8,256,256]{3,2,1,0:T(8,128)(2,1)} %bitcast.5, bf16[4,2,256,256]{3,2,1,0:T(8,128)(2,1)} %probe_h.1, f32[256,256]{1,0:T(8,128)} %phase_h.1, f32[2,256,256]{2,1,0:T(8,128)} %meas_h.1, bf16[512,256]{1,0:T(8,128)(2,1)} %constant.4.clone.tb_h, ...), custom_call_target="tpu_custom_call" | custom-call | tf_op jit(solution)/shard_map/ptycho/pallas_call | solution.py:507
  31.7 0.0 copy-done
  31.8 2.2 %assemble.1 = bf16[2,8,256,256]{3,2,1,0:T(8,128)(2,1)} custom-call(s32[2,256]{1,0:T(2,128)S(1)} %bitcast.4, bf16[4,2,256,256]{3,2,1,0:T(8,128)(2,1)S(1)} %ptycho.1.slots), custom_call_target="tpu_custom_call" | custom-call | tf_op jit(solution)/shard_map/assemble/pallas_call | solution.py:527
Async XLA Ops:
  0.0 31.7 %copy-start = (s32[256,2]{0,1:T(2,128)S(1)}, s32[256,2]{0,1:T(2,128)}, u32[]{:S(2)}) copy-start(s32[256,2]{0,1:T(2,128)} %param.11) | copy-start | bytes 6148

commit v9 on v8

--- a/solution.py
+++ b/solution.py
@@ -265,7 +265,7 @@
         k2 = jnp.minimum(k + 1, blocks - 1)
         a = band[part, k]
         b = band[part, k2]
-        return jnp.where(row_id >= (y & 255), a.astype(F32), b.astype(F32)).astype(BF)
+        return jnp.where(row_id >= (y & 255), a, b)
 
     loads[6].wait()
     loads[0].wait()
@@ -332,8 +332,7 @@
 
     def merge(s):
         for part in range(2):
-            ob[s, part] = jnp.where(near_mask, near[s, part].astype(F32),
-                                    farw[s, part].astype(F32))
+            ob[s, part] = jnp.where(near_mask, near[s, part], farw[s, part]).astype(F32)
 
     def bufs(m):
         return P.at[m % WIDTH], L.at[m % WIDTH]

time: 34 us -> 34 us (level)
  no operation moved by 1% of the time
where the time goes in v9:
time: 34 us; the launch traced here: 33.9 us
  Pallas kernels  33.9 us (100%)
    pallas_call x1, Pallas kernels, local(): pl.pallas_call(functools.partial(main_kernel, chips, height), out_shape=j...  31.7 us
    pallas_call x1, Pallas kernels, local(): pl.pallas_call(functools.partial(final_kernel, chips, blocks), out_shape=...  2.16 us

profile of v9, /device:TPU:6, one launch (start us, length us, event | category | flops | bytes accessed | tf_op | source)
XLA Modules:
  0.0 33.9 jit_solution(911746959527733564)
XLA Ops:
  0.0 0.0 copy-start
  0.0 31.7 %ptycho.1.slots = bf16[4,2,256,256]{3,2,1,0:T(8,128)(2,1)S(1)} custom-call(s32[2,256]{1,0:T(2,128)} %bitcast.3, bf16[2,8,256,256]{3,2,1,0:T(8,128)(2,1)} %bitcast.5, bf16[4,2,256,256]{3,2,1,0:T(8,128)(2,1)} %probe_h.1, f32[256,256]{1,0:T(8,128)} %phase_h.1, f32[2,256,256]{2,1,0:T(8,128)} %meas_h.1, bf16[512,256]{1,0:T(8,128)(2,1)} %constant.4.clone.tb_h, ...), custom_call_target="tpu_custom_call" | custom-call | tf_op jit(solution)/shard_map/ptycho/pallas_call | solution.py:506
  31.7 0.0 copy-done
  31.7 2.2 %assemble.1 = bf16[2,8,256,256]{3,2,1,0:T(8,128)(2,1)} custom-call(s32[2,256]{1,0:T(2,128)S(1)} %bitcast.4, bf16[4,2,256,256]{3,2,1,0:T(8,128)(2,1)S(1)} %ptycho.1.slots), custom_call_target="tpu_custom_call" | custom-call | tf_op jit(solution)/shard_map/assemble/pallas_call | solution.py:526
Async XLA Ops:
  0.0 31.7 %copy-start = (s32[256,2]{0,1:T(2,128)S(1)}, s32[256,2]{0,1:T(2,128)}, u32[]{:S(2)}) copy-start(s32[256,2]{0,1:T(2,128)} %param.11) | copy-start | bytes 6148
